TPU v7x, 32 devices: a whole 2x2x4 slice. The times are simulated.
32 devices in a mesh: seq: 4 (over z), shard: 8 (over y, x, core).
Axes of the slice: x: 2, y: 2, z: 4, core: 2. Of those that a mesh axis runs over, the one named last changes fastest.
Arguments:
- hidden_in: bfloat16 [8192, 512], P(('shard', 'seq')), may hold values from -6 to 6
- encoder: bfloat16 [2048, 512], P(('shard', 'seq')), may hold values from -6 to 6
- segment_ids: int32 [8192], replicated, may hold values from 0 to 1, never falling along the last dimension, each value on 1 to 5120 neighbouring positions
- timestep: int32 [2], replicated, may hold values from 0 to 49
- out_grad: bfloat16 [8192, 512], P(('shard', 'seq')), may hold values from -6 to 6
- time_table: bfloat16 [50, 512], P(None, 'shard'), may hold values from -6 to 6
- norm_gain: bfloat16 [3, 512], P(None, 'shard'), may hold values from 0.5 to 1.5
- norm_bias: bfloat16 [3, 512], P(None, 'shard'), may hold values from -1.5 to 1.5
- self_proj: bfloat16 [512, 1536], P('shard'), may hold values from -0.25 to 0.25
- self_out: bfloat16 [512, 512], P('shard'), may hold values from -1 to 1
- cross_query: bfloat16 [512, 512], P('shard'), may hold values from -0.25 to 0.25
- cross_memory: bfloat16 [512, 1024], P('shard'), may hold values from -0.25 to 0.25
- cross_out: bfloat16 [512, 512], P('shard'), may hold values from -1 to 1
- up_weight: bfloat16 [512, 2048], P('shard'), may hold values from -0.25 to 0.25
- up_bias: bfloat16 [2048], P('shard'), may hold values from -2.5 to 2.5
- down_weight: bfloat16 [2048, 512], P('shard'), may hold values from -0.125 to 0.125
- down_bias: bfloat16 [512], P('shard'), may hold values from -1.5 to 1.5
Outputs:
- layer_out: bfloat16 [8192, 512], P(('shard', 'seq'))
- hidden_grad: float32 [8192, 512], P(('shard', 'seq'))
- encoder_grad: float32 [2048, 512], P(('shard', 'seq'))
- time_grad: float32 [50, 512], P(None, 'shard')
- gain_grad: float32 [3, 512], P(None, 'shard')
- bias_grad: float32 [3, 512], P(None, 'shard')
- proj_grad: float32 [512, 1536], P('shard')
- self_out_grad: float32 [512, 512], P('shard')
- query_grad: float32 [512, 512], P('shard')
- memory_grad: float32 [512, 1024], P('shard')
- cross_out_grad: float32 [512, 512], P('shard')
- up_weight_grad: float32 [512, 2048], P('shard')
- up_bias_grad: float32 [2048], P('shard')
- down_weight_grad: float32 [2048, 512], P('shard')
- down_bias_grad: float32 [512], P('shard')
Inputs may be any that keep to these rules, and one draw needn't show every extreme that they name: `segment_ids`: never falling; 2 sequences of 1 to 5120 tokens each.
All inputs are finite; a program needn't handle non-finite values.
Results may differ from a plain program's by a relative error of at most 0.023.
Values may be sent and summed in bfloat16 or wider, within the bound.
A program may use at most 256 MiB of HBM per device.

v0:
```python
import jax
import jax.numpy as jnp
from jax import lax
from jax.sharding import PartitionSpec as P

D = 512
H = 8
HD = 64
DOCS = 2
ENC = 1024
STEPS = 50


highest = lax.Precision.HIGHEST
norm_eps = 1e-05
masked_score = -1e30


def layer_norm(value, gain, shift):
    center = jnp.mean(value, axis=-1, keepdims=True)
    offset = value - center
    spread = jnp.mean(offset * offset, axis=-1, keepdims=True)
    return offset * lax.rsqrt(spread + norm_eps) * gain + shift


def exact_gelu(value):
    return jax.nn.gelu(value, approximate=False)


def to_heads(stacked):
    return lax.all_to_all(stacked, "seq", split_axis=1, concat_axis=2, tiled=True)


def from_heads(stacked):
    return lax.all_to_all(stacked, "seq", split_axis=2, concat_axis=1, tiled=True)


def gather_keys(key_pair):
    return lax.all_gather(key_pair, "shard", axis=2, tiled=True)


def block_size(query_rows):
    return 2 * query_rows


def useful(segment_ids, key_first, key_count, query_first, query_count):
    last_seg = lax.dynamic_index_in_dim(segment_ids, key_first + key_count - 1, keepdims=False)
    first_seg = lax.dynamic_index_in_dim(segment_ids, query_first, keepdims=False)
    return (key_first <= query_first + query_count - 1) & (last_seg >= first_seg)


def score_block(key_block, key_first, context):
    queries, query_first, segment_ids = context
    query_rows = queries.shape[2]
    key_count = key_block.shape[2]
    raw_scores = jnp.einsum("hdq,hdk->hqk", queries, key_block, preferred_element_type=jnp.float32)
    query_seg = lax.dynamic_slice_in_dim(segment_ids, query_first, query_rows, 0)
    key_seg = lax.dynamic_slice_in_dim(segment_ids, key_first, key_count, 0)
    query_pos = query_first + jnp.arange(query_rows, dtype=jnp.int32)
    key_pos = key_first + jnp.arange(key_count, dtype=jnp.int32)
    allowed = (query_seg[:, None] == key_seg[None, :]) & (key_pos[None, :] <= query_pos[:, None])
    return jnp.where(allowed[None], HD ** (-0.5) * raw_scores, masked_score)


def fold_stats(carry_state, key_piece, context):
    queries, query_first, segment_ids = context
    head_local, head_size, query_rows = queries.shape
    row_count = key_piece.shape[1]
    block_rows = block_size(query_rows)
    key_all = key_piece.reshape(head_local, head_size, row_count)

    def turn(state_now, turn_index):
        local_first = turn_index * block_rows

        def work(state_in):
            row_top, row_total = state_in
            key_block = lax.dynamic_slice_in_dim(key_all, local_first, block_rows, 2)
            scores = score_block(key_block, local_first, context)
            new_top = jnp.maximum(row_top, jnp.max(scores, axis=2))
            new_total = row_total * jnp.exp(row_top - new_top) + jnp.sum(
                jnp.exp(scores - new_top[:, :, None]), axis=2
            )
            return (new_top, new_total)

        keep_on = useful(segment_ids, local_first, block_rows, query_first, query_rows)
        return (lax.cond(keep_on, work, lambda state_in: state_in, state_now), None)

    final_state, _ = lax.scan(
        turn, carry_state, jnp.arange(row_count // block_rows, dtype=jnp.int32)
    )
    return final_state


def fold_values(accum, pieces, context, log_total):
    queries, query_first, segment_ids = context
    head_local, head_size, query_rows = queries.shape
    row_count = pieces[0].shape[1]
    block_rows = block_size(query_rows)
    key_all = pieces[0].reshape(head_local, head_size, row_count)
    value_all = pieces[1].reshape(head_local, head_size, row_count)

    def turn(accum_now, turn_index):
        local_first = turn_index * block_rows

        def work(accum_in):
            key_block = lax.dynamic_slice_in_dim(key_all, local_first, block_rows, 2)
            value_block = lax.dynamic_slice_in_dim(value_all, local_first, block_rows, 2)
            scores = score_block(key_block, local_first, context)
            attn_probs = jnp.exp(scores - log_total[:, :, None]).astype(jnp.bfloat16)
            return accum_in + jnp.einsum(
                "hqk,hdk->hdq", attn_probs, value_block, preferred_element_type=jnp.float32
            )

        keep_on = useful(segment_ids, local_first, block_rows, query_first, query_rows)
        return (lax.cond(keep_on, work, lambda accum_in: accum_in, accum_now), None)

    final_accum, _ = lax.scan(turn, accum, jnp.arange(row_count // block_rows, dtype=jnp.int32))
    return final_accum


def attention_grads(key_pair, grad_heads, log_total, row_delta, context):
    queries, query_first, segment_ids = context
    head_local, head_size, query_rows = queries.shape
    row_count = key_pair.shape[2]
    block_rows = block_size(query_rows)
    key_all = key_pair.reshape(2, head_local, head_size, row_count)
    scale_factor = HD ** (-0.5)

    def turn(carry_state, turn_index):
        key_first = turn_index * block_rows

        def work(state_in):
            d_query, key_terms = state_in
            key_block = lax.dynamic_slice_in_dim(key_all[0], key_first, block_rows, 2)
            value_block = lax.dynamic_slice_in_dim(key_all[1], key_first, block_rows, 2)
            scores = score_block(key_block, key_first, context)
            attn_probs = jnp.exp(scores - log_total[:, :, None])
            d_probs = jnp.einsum(
                "hdq,hdk->hqk", grad_heads, value_block, preferred_element_type=jnp.float32
            )
            d_raw = (scale_factor * attn_probs * (d_probs - row_delta[:, :, None])).astype(
                jnp.bfloat16
            )
            d_query = d_query + jnp.einsum(
                "hqk,hdk->hdq", d_raw, key_block, preferred_element_type=jnp.float32
            )
            d_key = jnp.einsum("hqk,hdq->hdk", d_raw, queries, preferred_element_type=jnp.float32)
            d_value = jnp.einsum(
                "hqk,hdq->hdk",
                attn_probs.astype(jnp.bfloat16),
                grad_heads,
                preferred_element_type=jnp.float32,
            )
            key_terms = lax.dynamic_update_slice_in_dim(
                key_terms, jnp.stack([d_key, d_value]), key_first, 3
            )
            return (d_query, key_terms)

        keep_on = useful(segment_ids, key_first, block_rows, query_first, query_rows)
        return (lax.cond(keep_on, work, lambda state_in: state_in, carry_state), None)

    start_state = (
        jnp.zeros((head_local, head_size, query_rows), jnp.float32),
        jnp.zeros((2, head_local, head_size, row_count), jnp.float32),
    )
    final_state, _ = lax.scan(
        turn, start_state, jnp.arange(row_count // block_rows, dtype=jnp.int32)
    )
    return (final_state[0], final_state[1].reshape(2, head_local * head_size, row_count))


def cross_forward_doc(carry_state, doc_keys, doc_values, in_doc, cross_queries):
    accum, log_acc = carry_state
    raw_scores = jnp.einsum(
        "hdq,hdk->hqk", cross_queries, doc_keys, preferred_element_type=jnp.float32
    )
    scores = HD ** (-0.5) * raw_scores
    row_top = jnp.max(scores, axis=2)
    powers = jnp.exp(scores - row_top[:, :, None])
    row_total = jnp.sum(powers, axis=2)
    attn_probs = (powers / row_total[:, :, None]).astype(jnp.bfloat16)
    result = jnp.einsum("hqk,hdk->hdq", attn_probs, doc_values, preferred_element_type=jnp.float32)
    accum = jnp.where(in_doc[None, None, :], result, accum)
    log_acc = jnp.where(in_doc[None, :], row_top + jnp.log(row_total), log_acc)
    return (accum, log_acc)


def cross_backward_doc(
    carry_state,
    doc_keys,
    doc_values,
    in_doc,
    cross_queries,
    grad_cross,
    cross_log,
    cross_delta,
    doc_first,
):
    d_query, key_terms = carry_state
    raw_scores = jnp.einsum(
        "hdq,hdk->hqk", cross_queries, doc_keys, preferred_element_type=jnp.float32
    )
    scores = HD ** (-0.5) * raw_scores
    attn_probs = jnp.where(in_doc[None, :, None], jnp.exp(scores - cross_log[:, :, None]), 0.0)
    d_probs = jnp.einsum("hdq,hdk->hqk", grad_cross, doc_values, preferred_element_type=jnp.float32)
    d_raw = (HD ** (-0.5) * attn_probs * (d_probs - cross_delta[:, :, None])).astype(jnp.bfloat16)
    d_query = d_query + jnp.einsum(
        "hqk,hdk->hdq", d_raw, doc_keys, preferred_element_type=jnp.float32
    )
    d_key = jnp.einsum("hqk,hdq->hdk", d_raw, cross_queries, preferred_element_type=jnp.float32)
    d_value = jnp.einsum(
        "hqk,hdq->hdk",
        attn_probs.astype(jnp.bfloat16),
        grad_cross,
        preferred_element_type=jnp.float32,
    )
    key_terms = lax.dynamic_update_slice_in_dim(
        key_terms, jnp.stack([d_key, d_value]), doc_first, 3
    )
    return (d_query, key_terms)


def shards(
    hidden_in,
    encoder,
    segment_ids,
    timestep,
    out_grad,
    time_table,
    norm_gain,
    norm_bias,
    self_proj,
    self_out,
    cross_query,
    cross_memory,
    cross_out,
    up_weight,
    up_bias,
    down_weight,
    down_bias,
):
    seq_count = lax.axis_size("seq")
    shard_pos = lax.axis_index("shard")
    seq_pos = lax.axis_index("seq")
    local_rows = hidden_in.shape[0]
    enc_local = encoder.shape[0]
    query_rows = local_rows * seq_count
    head_local = H // seq_count
    token_first = (shard_pos * seq_count + seq_pos) * local_rows
    query_first = shard_pos * query_rows
    gathered = (
        lax.all_gather(time_table, "shard", axis=1, tiled=True),
        lax.all_gather(norm_gain, "shard", axis=1, tiled=True),
        lax.all_gather(norm_bias, "shard", axis=1, tiled=True),
        lax.all_gather(self_proj, "shard", axis=0, tiled=True),
        lax.all_gather(self_out, "shard", axis=0, tiled=True),
        lax.all_gather(cross_query, "shard", axis=0, tiled=True),
        lax.all_gather(cross_memory, "shard", axis=0, tiled=True),
        lax.all_gather(cross_out, "shard", axis=0, tiled=True),
        lax.all_gather(up_weight, "shard", axis=0, tiled=True),
        lax.all_gather(up_bias, "shard", axis=0, tiled=True),
        lax.all_gather(down_weight, "shard", axis=0, tiled=True),
        lax.all_gather(down_bias, "shard", axis=0, tiled=True),
    )
    (
        table_all,
        gain_all,
        bias_all,
        proj_all,
        out_all,
        query_all,
        memory_all,
        cout_all,
        up_all,
        upb_all,
        down_all,
        downb_all,
    ) = gathered
    local_seg = lax.dynamic_slice_in_dim(segment_ids, token_first, local_rows, 0)
    doc_hot = (local_seg[:, None] == jnp.arange(DOCS, dtype=jnp.int32)[None, :]).astype(jnp.float32)
    step_hot = (timestep[:, None] == jnp.arange(STEPS, dtype=jnp.int32)[None, :]).astype(
        jnp.float32
    )
    doc_embed = jnp.dot(step_hot, table_all.astype(jnp.float32), precision=highest)
    embedded = hidden_in.astype(jnp.float32) + jnp.dot(doc_hot, doc_embed, precision=highest)
    gains = gain_all.astype(jnp.float32)
    shifts = bias_all.astype(jnp.float32)
    normed_one, norm_back_one = jax.vjp(layer_norm, embedded, gains[0], shifts[0])
    normed_one = normed_one.astype(jnp.bfloat16)
    proj_t = jnp.einsum("td,de->et", normed_one, proj_all, preferred_element_type=jnp.float32)
    self_heads = to_heads(proj_t.astype(jnp.bfloat16).reshape(3, D, local_rows))
    queries = self_heads[0].reshape(head_local, HD, query_rows)
    context = (queries, query_first, segment_ids)
    query_seg = lax.dynamic_slice_in_dim(segment_ids, query_first, query_rows, 0)
    row_top = jnp.full((head_local, query_rows), masked_score, jnp.float32)
    row_total = jnp.zeros((head_local, query_rows), jnp.float32)
    accum = jnp.zeros((head_local, HD, query_rows), jnp.float32)
    row_top, row_total = fold_stats(
        (row_top, row_total), lax.all_gather(self_heads[1], "shard", axis=1, tiled=True), context
    )
    log_total = row_top + jnp.log(row_total)
    accum = fold_values(
        accum,
        (
            lax.all_gather(self_heads[1], "shard", axis=1, tiled=True),
            lax.all_gather(self_heads[2], "shard", axis=1, tiled=True),
        ),
        context,
        log_total,
    )
    attn_t = from_heads(accum.astype(jnp.bfloat16).reshape(1, head_local * HD, query_rows))[0]
    after = embedded + jnp.einsum("et,ef->tf", attn_t, out_all, preferred_element_type=jnp.float32)
    normed_two, norm_back_two = jax.vjp(layer_norm, after, gains[1], shifts[1])
    normed_two = normed_two.astype(jnp.bfloat16)
    cross_q_t = jnp.einsum("td,de->et", normed_two, query_all, preferred_element_type=jnp.float32)
    cross_queries = to_heads(cross_q_t.astype(jnp.bfloat16)[None])[0].reshape(
        head_local, HD, query_rows
    )
    memory_t = jnp.einsum("td,de->et", encoder, memory_all, preferred_element_type=jnp.float32)
    memory_heads = to_heads(memory_t.astype(jnp.bfloat16).reshape(2, D, enc_local))
    memory_keys = lax.all_gather(memory_heads, "shard", axis=2, tiled=True)
    enc_total = memory_keys.shape[2]
    memory_keys = memory_keys.reshape(2, head_local, HD, enc_total)
    cross_state = (
        jnp.zeros((head_local, HD, query_rows), jnp.float32),
        jnp.zeros((head_local, query_rows), jnp.float32),
    )
    for doc_number in range(DOCS):
        in_doc = query_seg == doc_number
        doc_keys = memory_keys[0, :, :, doc_number * ENC : (doc_number + 1) * ENC]
        doc_values = memory_keys[1, :, :, doc_number * ENC : (doc_number + 1) * ENC]
        cross_state = lax.cond(
            jnp.any(in_doc),
            lambda state_in, doc_keys=doc_keys, doc_values=doc_values, in_doc=in_doc: cross_forward_doc(
                state_in, doc_keys, doc_values, in_doc, cross_queries
            ),
            lambda state_in: state_in,
            cross_state,
        )
    cross_accum, cross_log = cross_state
    cross_t = from_heads(cross_accum.astype(jnp.bfloat16).reshape(1, head_local * HD, query_rows))[
        0
    ]
    after_two = after + jnp.einsum(
        "et,ef->tf", cross_t, cout_all, preferred_element_type=jnp.float32
    )
    normed_three, norm_back_three = jax.vjp(layer_norm, after_two, gains[2], shifts[2])
    normed_three = normed_three.astype(jnp.bfloat16)
    pre_act = jnp.einsum("td,df->tf", normed_three, up_all, preferred_element_type=jnp.float32)
    pre_act = pre_act + upb_all.astype(jnp.float32)
    middle, gelu_back = jax.vjp(exact_gelu, pre_act)
    middle = middle.astype(jnp.bfloat16)
    ffn_branch = jnp.einsum("tf,fd->td", middle, down_all, preferred_element_type=jnp.float32)
    layer_out = (after_two + ffn_branch + downb_all.astype(jnp.float32)).astype(jnp.bfloat16)
    grad_top = out_grad.astype(jnp.float32)
    down_grad = jnp.einsum("tf,td->fd", middle, out_grad, preferred_element_type=jnp.float32)
    down_bias_grad = jnp.sum(grad_top, axis=0)
    d_middle = jnp.einsum("td,fd->tf", out_grad, down_all, preferred_element_type=jnp.float32)
    d_pre = gelu_back(d_middle)[0].astype(jnp.bfloat16)
    up_grad = jnp.einsum("td,tf->df", normed_three, d_pre, preferred_element_type=jnp.float32)
    up_bias_grad = jnp.sum(d_pre.astype(jnp.float32), axis=0)
    d_normed_three = jnp.einsum("tf,df->td", d_pre, up_all, preferred_element_type=jnp.float32)
    d_after_part, gain_three, shift_three = norm_back_three(d_normed_three)
    d_after_two = grad_top + d_after_part
    d_cross_in = d_after_two.astype(jnp.bfloat16)
    cross_out_grad = jnp.einsum(
        "et,tf->ef", cross_t, d_cross_in, preferred_element_type=jnp.float32
    )
    d_cross_t = jnp.einsum("ef,tf->et", cout_all, d_cross_in, preferred_element_type=jnp.float32)
    grad_cross = to_heads(d_cross_t.astype(jnp.bfloat16)[None])[0].reshape(
        head_local, HD, query_rows
    )
    cross_delta = jnp.sum(grad_cross.astype(jnp.float32) * cross_accum, axis=1)
    cross_grad_state = (
        jnp.zeros((head_local, HD, query_rows), jnp.float32),
        jnp.zeros((2, head_local, HD, enc_total), jnp.float32),
    )
    for doc_number in range(DOCS):
        in_doc = query_seg == doc_number
        doc_keys = memory_keys[0, :, :, doc_number * ENC : (doc_number + 1) * ENC]
        doc_values = memory_keys[1, :, :, doc_number * ENC : (doc_number + 1) * ENC]
        cross_grad_state = lax.cond(
            jnp.any(in_doc),
            lambda state_in, doc_keys=doc_keys, doc_values=doc_values, in_doc=in_doc, doc_number=doc_number: cross_backward_doc(
                state_in,
                doc_keys,
                doc_values,
                in_doc,
                cross_queries,
                grad_cross,
                cross_log,
                cross_delta,
                doc_number * ENC,
            ),
            lambda state_in: state_in,
            cross_grad_state,
        )
    d_cross_query, cross_terms = cross_grad_state
    cross_terms = cross_terms.reshape(2, head_local * HD, enc_total)
    d_cq_t = from_heads(d_cross_query.astype(jnp.bfloat16).reshape(1, head_local * HD, query_rows))[
        0
    ]
    query_grad = jnp.einsum("td,et->de", normed_two, d_cq_t, preferred_element_type=jnp.float32)
    d_normed_two = jnp.einsum("de,et->td", query_all, d_cq_t, preferred_element_type=jnp.float32)
    d_after_cross, gain_two, shift_two = norm_back_two(d_normed_two)
    d_after = d_after_two + d_after_cross
    d_attn_in = d_after.astype(jnp.bfloat16)
    self_out_grad = jnp.einsum("et,tf->ef", attn_t, d_attn_in, preferred_element_type=jnp.float32)
    d_attn_t = jnp.einsum("ef,tf->et", out_all, d_attn_in, preferred_element_type=jnp.float32)
    grad_heads = to_heads(d_attn_t.astype(jnp.bfloat16)[None])[0].reshape(
        head_local, HD, query_rows
    )
    row_delta = jnp.sum(grad_heads.astype(jnp.float32) * accum, axis=1)
    key_pair = gather_keys(self_heads[1:])
    d_self_query, self_terms = attention_grads(key_pair, grad_heads, log_total, row_delta, context)
    self_kv, cross_kv = (
        lax.psum_scatter(
            self_terms.astype(jnp.bfloat16), "shard", scatter_dimension=2, tiled=True
        ).astype(jnp.float32),
        lax.psum_scatter(
            cross_terms.astype(jnp.bfloat16), "shard", scatter_dimension=2, tiled=True
        ).astype(jnp.float32),
    )
    self_grads = jnp.concatenate(
        [d_self_query.reshape(1, head_local * HD, query_rows), self_kv], axis=0
    ).astype(jnp.bfloat16)
    home_self, home_cross = (
        lax.all_to_all(self_grads, "seq", split_axis=2, concat_axis=1, tiled=True),
        lax.all_to_all(
            cross_kv.astype(jnp.bfloat16), "seq", split_axis=2, concat_axis=1, tiled=True
        ),
    )
    d_proj_t = home_self.reshape(3 * D, local_rows)
    proj_grad = jnp.einsum("td,et->de", normed_one, d_proj_t, preferred_element_type=jnp.float32)
    d_normed_one = jnp.einsum("de,et->td", proj_all, d_proj_t, preferred_element_type=jnp.float32)
    d_embed_part, gain_one, shift_one = norm_back_one(d_normed_one)
    hidden_grad = d_after + d_embed_part
    d_memory_t = home_cross.reshape(2 * D, enc_local)
    memory_grad = jnp.einsum("td,et->de", encoder, d_memory_t, preferred_element_type=jnp.float32)
    encoder_grad = jnp.einsum(
        "de,et->td", memory_all, d_memory_t, preferred_element_type=jnp.float32
    )
    doc_grad = jnp.einsum("tc,td->cd", doc_hot, hidden_grad, precision=highest)
    time_grad = jnp.einsum("cs,cd->sd", step_hot, doc_grad, precision=highest)
    gain_grad = jnp.stack([gain_one, gain_two, gain_three])
    bias_grad = jnp.stack([shift_one, shift_two, shift_three])
    shares = (
        lax.psum_scatter(
            time_grad.astype(jnp.bfloat16), "shard", scatter_dimension=1, tiled=True
        ).astype(jnp.float32),
        lax.psum_scatter(
            gain_grad.astype(jnp.bfloat16), "shard", scatter_dimension=1, tiled=True
        ).astype(jnp.float32),
        lax.psum_scatter(
            bias_grad.astype(jnp.bfloat16), "shard", scatter_dimension=1, tiled=True
        ).astype(jnp.float32),
        lax.psum_scatter(
            proj_grad.astype(jnp.bfloat16), "shard", scatter_dimension=0, tiled=True
        ).astype(jnp.float32),
        lax.psum_scatter(
            self_out_grad.astype(jnp.bfloat16), "shard", scatter_dimension=0, tiled=True
        ).astype(jnp.float32),
        lax.psum_scatter(
            query_grad.astype(jnp.bfloat16), "shard", scatter_dimension=0, tiled=True
        ).astype(jnp.float32),
        lax.psum_scatter(
            memory_grad.astype(jnp.bfloat16), "shard", scatter_dimension=0, tiled=True
        ).astype(jnp.float32),
        lax.psum_scatter(
            cross_out_grad.astype(jnp.bfloat16), "shard", scatter_dimension=0, tiled=True
        ).astype(jnp.float32),
        lax.psum_scatter(
            up_grad.astype(jnp.bfloat16), "shard", scatter_dimension=0, tiled=True
        ).astype(jnp.float32),
        lax.psum_scatter(
            up_bias_grad.astype(jnp.bfloat16), "shard", scatter_dimension=0, tiled=True
        ).astype(jnp.float32),
        lax.psum_scatter(
            down_grad.astype(jnp.bfloat16), "shard", scatter_dimension=0, tiled=True
        ).astype(jnp.float32),
        lax.psum_scatter(
            down_bias_grad.astype(jnp.bfloat16), "shard", scatter_dimension=0, tiled=True
        ).astype(jnp.float32),
    )
    (
        time_part,
        gain_part,
        bias_part,
        proj_part,
        out_part,
        query_part,
        memory_part,
        cout_part,
        up_part,
        upb_part,
        down_part,
        downb_part,
    ) = shares
    totals = (
        lax.psum(time_part.astype(jnp.bfloat16), "seq").astype(jnp.float32),
        lax.psum(gain_part.astype(jnp.bfloat16), "seq").astype(jnp.float32),
        lax.psum(bias_part.astype(jnp.bfloat16), "seq").astype(jnp.float32),
        lax.psum(proj_part.astype(jnp.bfloat16), "seq").astype(jnp.float32),
        lax.psum(out_part.astype(jnp.bfloat16), "seq").astype(jnp.float32),
        lax.psum(query_part.astype(jnp.bfloat16), "seq").astype(jnp.float32),
        lax.psum(memory_part.astype(jnp.bfloat16), "seq").astype(jnp.float32),
        lax.psum(cout_part.astype(jnp.bfloat16), "seq").astype(jnp.float32),
        lax.psum(up_part.astype(jnp.bfloat16), "seq").astype(jnp.float32),
        lax.psum(upb_part.astype(jnp.bfloat16), "seq").astype(jnp.float32),
        lax.psum(down_part.astype(jnp.bfloat16), "seq").astype(jnp.float32),
        lax.psum(downb_part.astype(jnp.bfloat16), "seq").astype(jnp.float32),
    )
    return (
        layer_out,
        hidden_grad,
        encoder_grad,
        totals[0],
        totals[1],
        totals[2],
        totals[3],
        totals[4],
        totals[5],
        totals[6],
        totals[7],
        totals[8],
        totals[9],
        totals[10],
        totals[11],
    )


def solution(mesh):
    return jax.shard_map(
        shards,
        mesh=mesh,
        in_specs=(
            P(("shard", "seq"), None),
            P(("shard", "seq"), None),
            P(),
            P(),
            P(("shard", "seq"), None),
            P(None, "shard"),
            P(None, "shard"),
            P(None, "shard"),
            P("shard", None),
            P("shard", None),
            P("shard", None),
            P("shard", None),
            P("shard", None),
            P("shard", None),
            P("shard"),
            P("shard", None),
            P("shard"),
        ),
        out_specs=(
            P(("shard", "seq"), None),
            P(("shard", "seq"), None),
            P(("shard", "seq"), None),
            P(None, "shard"),
            P(None, "shard"),
            P(None, "shard"),
            P("shard", None),
            P("shard", None),
            P("shard", None),
            P("shard", None),
            P("shard", None),
            P("shard", None),
            P("shard"),
            P("shard", None),
            P("shard"),
        ),
        check_vma=False,
    )
```

profile of v0, /device:TPU:0, one launch (start us, length us, event | category | flops | bytes accessed | tf_op | source)
XLA Modules:
  0.0 1110.8 jit_solution(14375068837546095418)
XLA Ops:
  44.4 30.8 %all_to_all.153 = bf16[3,512,256]{2,0,1:T(4,128)(2,1)S(1)} all-to-all(bf16[3,512,256]{2,0,1:T(4,128)(2,1)S(1)} %copy.265), channel_id=1, replica_groups=mesh['seq'=4,'shard'=8] {'seq'}, dimensions={1} | all-to-all | bytes 1572864 | tf_op jit(solution)/shard_map/all_to_all | solution.py:31
  107.5 26.1 %all-gather.15.cloned.1.call-done = bf16[128,8192]{0,1:T(8,128)(2,1)} async-done(((bf16[128,1024]{0,1:T(8,128)(2,1)}), bf16[128,8192]{0,1:T(8,128)(2,1)}) %all-gather.15.cloned.1.call-update) | async-done | bytes 2097168 | tf_op jit(solution)/shard_map/all_gather | solution.py:306
  137.8 24.1 %while.52 = (s32[]{:T(128)}, f32[2,1024]{1,0:T(2,128)S(1)}, f32[2,1024]{1,0:T(2,128)S(1)}, s32[4]{0:T(128)S(1)}, s32[]{:T(128)}, /*index=5*/s32[8192]{0:T(1024)S...) while((s32[]{:T(128)}, f32[2,1024]{1,0:T(2,128)S(1)}, ...), condition=%wide.region_7.8_spmd, body=%wide.region_2.7_spmd.sunk | while | flops 572529664 | bytes 40800696 | solution.py:88
  140.9 11.5 %conditional.14 = ((f32[2,1024]{1,0:T(2,128)S(1)}, f32[2,1024]{1,0:T(2,128)S(1)})) conditional(s32[]{:T(128)} %convert_element_type.405, (f32[2,1024]{1,0:T(2,128)S(1)}, f32[2,1024]{1,0:T(2,128)S(1)}) %tuple.215, (s32[]{:T(128)}, s32[8192]{0:T(1024)S(1)}, s32[]{:T(128)}, bf16[2,64,8192]{2,1,0:T(8,128)(2,1)}, bf16[2,64,1024]{2,1,0:T(8,128)(2,1)S(1)}, ...), branch_computations={%region_3.3_spmd, %region_4.6_spmd} | conditional | flops 572529664 | bytes 40800368 | solution.py:86
  162.0 22.5 %while.53 = (s32[]{:T(128)}, f32[2,64,1024]{2,1,0:T(8,128)S(1)}, s32[4]{0:T(128)S(1)}, s32[]{:T(128)}, s32[8192]{0:T(1024)S(1)}, /*index=5*/s32[1]{0:T(128)}, bf...) while((s32[]{:T(128)}, f32[2,64,1024]{2,1,0:T(8,128)S(1)}, ...), condition=%wide.region_11.12_spmd, body=%wide.region_8.11_spmd.sunk | while | flops 1096944640 | bytes 6624677 | solution.py:117
  195.6 52.4 %all_gather.55 = bf16[512,512]{1,0:T(8,128)(2,1)S(1)} all-gather(bf16[64,512]{1,0:T(8,128)(2,1)S(1)} %copy-done.36), channel_id=1, replica_groups=mesh['seq'=4,'shard'=8] {'shard'}, dimensions={0}, use_global_device_ids=true | all-gather | bytes 589824 | tf_op jit(solution)/shard_map/all_gather | solution.py:256
  293.2 13.3 %all-gather.3 = bf16[8,1,256]{2,1,0:T(2,128)(2,1)S(1)} all-gather(bf16[1,1,256]{2,1,0:T(2,128)(2,1)S(1)} %reshape.438), channel_id=1, replica_groups=mesh['seq'=4,'shard'=8] {'shard'}, dimensions={0}, use_global_device_ids=true | all-gather | bytes 4608 | tf_op jit(solution)/shard_map/all_gather | solution.py:261
  361.7 13.2 %conditional.9 = (f32[2,64,1024]{2,1,0:T(8,128)S(1)}, bf16[2,2,64,2048]{3,2,1,0:T(8,128)(2,1)}) conditional(s32[]{:T(128)} %convert_element_type.268, () %tuple.137, (pred[1024]{0:T(1024)(128)(4,1)}, bf16[2,64,1024]{2,1,0:T(8,128)(2,1)S(1)}, bf16[2,64,1024]{2,1,0:T(8,128)(2,1)}, f32[2,1024]{1,0:T(2,128)S(1)}, bf16[2,64,1024]{2,1,0:T(8,128)(2,1)S(1)}, ...), branch_computations={%region_29.30_spmd, %region_30.31_spmd} | conditional | flops 1368915968 | bytes 43280428 | solution.py:382
  420.2 60.7 %while.54 = (s32[]{:T(128)}, f32[2,64,1024]{2,1,0:T(8,128)S(1)}, bf16[2,2,64,8192]{3,2,1,0:T(8,128)(2,1)}, s32[4]{0:T(128)S(1)}, s32[]{:T(128)}, /*index=5*/s32[...) while((s32[]{:T(128)}, f32[2,64,1024]{2,1,0:T(8,128)S(1)}, ...), condition=%wide.region_39.40_spmd, body=%wide.region_36.39_spmd.sunk | while | flops 2737441792 | bytes 166285824 | solution.py:166
  423.5 47.8 %conditional.16 = ((f32[2,64,1024]{2,1,0:T(8,128)S(1)}, bf16[2,2,64,8192]{3,2,1,0:T(8,128)(2,1)})) conditional(s32[]{:T(128)} %convert_element_type.407, (f32[2,64,1024]{2,1,0:T(8,128)S(1)}, bf16[2,2,64,8192]{3,2,1,0:T(8,128)(2,1)}) %tuple.220, (bf16[2,2,64,8192]{3,2,1,0:T(8,128)(2,1)}, s32[]{:T(128)}, s32[]{:T(128)}, s32[8192]{0:T(1024)S(1)}, ...), branch_computations={%region_37.37_spmd, %region_38.38_spmd} | conditional | flops 2737441792 | bytes 166285440 | solution.py:160
  507.8 127.6 %reduce-scatter.21.cloned.1.call-done = bf16[2,128,1024]{2,1,0:T(8,128)(2,1)} async-done(((bf16[2,128,8192]{2,1,0:T(8,128)(2,1)}), bf16[2,128,1024]{2,1,0:T(8,128)(2,1)}) %reduce-scatter.21.cloned.1.call-update) | async-done | bytes 524304 | tf_op jit(solution)/shard_map/reduce_scatter | solution.py:417
  639.9 30.3 %all_to_all.156 = bf16[3,128,1024]{1,0,2:T(4,128)(2,1)S(1)} all-to-all(bf16[3,128,1024]{1,0,2:T(4,128)(2,1)} %copy.290), channel_id=1, replica_groups=mesh['seq'=4,'shard'=8] {'seq'}, dimensions={2} | all-to-all | bytes 1572864 | tf_op jit(solution)/shard_map/all_to_all | solution.py:428
  686.6 25.8 %reduce-scatter.31.cloned.1.call-done = bf16[64,512]{1,0:T(8,128)(2,1)} async-done(((bf16[512,512]{1,0:T(8,128)(2,1)}), bf16[64,512]{1,0:T(8,128)(2,1)}) %reduce-scatter.31.cloned.1.call-update) | async-done | bytes 65552 | tf_op jit(solution)/shard_map/reduce_scatter | solution.py:469
  712.5 37.2 %reduce-scatter.29.cloned.1.call-done = bf16[64,512]{1,0:T(8,128)(2,1)} async-done(((bf16[512,512]{1,0:T(8,128)(2,1)}), bf16[64,512]{1,0:T(8,128)(2,1)}) %reduce-scatter.29.cloned.1.call-update) | async-done | bytes 65552 | tf_op jit(solution)/shard_map/reduce_scatter | solution.py:463
  749.6 38.0 %reduce-scatter.27.cloned.1.call-done = bf16[64,512]{1,0:T(8,128)(2,1)} async-done(((bf16[512,512]{1,0:T(8,128)(2,1)}), bf16[64,512]{1,0:T(8,128)(2,1)}) %reduce-scatter.27.cloned.1.call-update) | async-done | bytes 65552 | tf_op jit(solution)/shard_map/reduce_scatter | solution.py:460
  787.7 44.3 %reduce-scatter.33.cloned.1.call-done = bf16[64,2048]{1,0:T(8,128)(2,1)} async-done(((bf16[512,2048]{1,0:T(8,128)(2,1)}), bf16[64,2048]{1,0:T(8,128)(2,1)}) %reduce-scatter.33.cloned.1.call-update) | async-done | bytes 262160 | tf_op jit(solution)/shard_map/reduce_scatter | solution.py:472
  832.0 44.8 %reduce-scatter.35.cloned.1.call-done = bf16[256,512]{1,0:T(8,128)(2,1)} async-done(((bf16[2048,512]{1,0:T(8,128)(2,1)}), bf16[256,512]{1,0:T(8,128)(2,1)}) %reduce-scatter.35.cloned.1.call-update) | async-done | bytes 262160 | tf_op jit(solution)/shard_map/reduce_scatter | solution.py:478
  876.8 41.6 %reduce-scatter.25.cloned.1.call-done = bf16[64,1536]{1,0:T(8,128)(2,1)} async-done(((bf16[512,1536]{1,0:T(8,128)(2,1)}), bf16[64,1536]{1,0:T(8,128)(2,1)}) %reduce-scatter.25.cloned.1.call-update) | async-done | bytes 196624 | tf_op jit(solution)/shard_map/reduce_scatter | solution.py:457
  921.3 13.0 %all-reduce.4 = (bf16[512]{0:T(512)(128)(2,1)S(1)}, bf16[2048]{0:T(1024)(128)(2,1)S(1)}, bf16[512]{0:T(512)(128)(2,1)S(1)}) all-reduce(bf16[512]{0:T(512)(128)(2,1)S(1)} %dynamic-update-slice, bf16[2048]{0:T(1024)(128)(2,1)S(1)} %copy-done.74, bf16[512]{0:T(512)(128)(2,1)S(1)} %reduce_sum.300), channel_id=1, replica_groups=mesh['seq'=4,'shard'=8] {'shard'}, use_global_device_ids=true, to_apply=%add.1 | all-reduce | flops 3072 | bytes 12288
  939.8 15.4 %reduce-scatter.41.cloned.1.call-done = bf16[64,3]{1,0:T(8,128)(2,1)} async-done(((bf16[512,3]{1,0:T(8,128)(2,1)}), bf16[64,3]{1,0:T(8,128)(2,1)}) %reduce-scatter.41.cloned.1.call-update) | async-done | bytes 400
  956.0 36.5 %reduce-scatter.39.cloned.1.call-done = bf16[64,3]{1,0:T(8,128)(2,1)} async-done(((bf16[512,3]{1,0:T(8,128)(2,1)}), bf16[64,3]{1,0:T(8,128)(2,1)}) %reduce-scatter.39.cloned.1.call-update) | async-done | bytes 400
  993.2 36.0 %reduce-scatter.37.cloned.1.call-done = bf16[64,50]{1,0:T(8,128)(2,1)} async-done(((bf16[512,50]{1,0:T(8,128)(2,1)}), bf16[64,50]{1,0:T(8,128)(2,1)}) %reduce-scatter.37.cloned.1.call-update) | async-done | bytes 6416
  1030.1 19.5 %all-reduce.5 = (bf16[50,64]{1,0:T(8,128)(2,1)S(1)}, bf16[3,64]{1,0:T(4,128)(2,1)S(1)}, bf16[3,64]{1,0:T(4,128)(2,1)S(1)}, bf16[256]{0:T(256)(128)(2,1)S(1)}, bf16[64]{0:T(256)(128)(2,1)S(1)}) all-reduce(bf16[50,64]{1,0:T(8,128)(2,1)S(1)} %copy.305, bf16[3,64]{1,0:T(4,128)(2,1)S(1)} %copy.307, ...), channel_id=1, replica_groups=mesh['seq'=4,'shard'=8] {'seq'}, use_global_device_ids=true, to_apply=%region_45.46 | all-reduce | flops 3904 | bytes 15616 | tf_op jit(solution)/shard_map/psum | solution.py:500
  1052.5 39.7 %all-reduce.9.cloned.1.call-done = (bf16[64,1024]{0,1:T(8,128)(2,1)}, bf16[64,1536]{1,0:T(8,128)(2,1)}, bf16[64,512]{1,0:T(8,128)(2,1)}, bf16[64,512]{1,0:T(8,12...) async-done(((bf16[64,1024]{0,1:T(8,128)(2,1)}, bf16[64,1536]{1,0:T(8,128)(2,1)}, bf16[64,512]{1,0:T(8,128)(2,1)}, ...) | async-done | bytes 1048592 | tf_op jit(solution)/shard_map/psum | solution.py:506
  (485 shorter events, 411.3 us)
Async XLA Ops:
  7.2 34.2 %all-gather.13.cloned.1.call-start = ((), (), s32[]{:S(2)}) async-start(), calls=%async_computation.22 | async-start | bytes 1769472 | tf_op jit(solution)/shard_map/all_gather | solution.py:255
  7.9 70.2 %all-gather.19.cloned.1.call-start = ((), (), s32[]{:S(2)}) async-start(), calls=%async_computation.25 | async-start | bytes 1179648 | tf_op jit(solution)/shard_map/all_gather | solution.py:258
  8.7 94.7 %all-gather.17.cloned.1.call-start = ((), (), s32[]{:S(2)}) async-start(), calls=%async_computation.24 | async-start | bytes 2359296 | tf_op jit(solution)/shard_map/all_gather | solution.py:305
  77.2 56.5 %all-gather.15.cloned.1.call-start = ((), (), s32[]{:S(2)}) async-start(), calls=%async_computation.23 | async-start | bytes 2359296 | tf_op jit(solution)/shard_map/all_gather | solution.py:306
  78.1 192.4 %all-gather.21.cloned.1.call-start = ((), (), s32[]{:S(2)}) async-start(), calls=%async_computation.26 | async-start | bytes 1179648 | tf_op jit(solution)/shard_map/all_gather | solution.py:321
  89.8 232.7 %all-gather.23.cloned.1.call-start = ((), (), s32[]{:S(2)}) async-start(), calls=%async_computation.27 | async-start | bytes 2359296 | tf_op jit(solution)/shard_map/all_gather | solution.py:260
  90.4 235.9 %all-gather.25.cloned.1.call-start = ((), (), s32[]{:S(2)}) async-start(), calls=%async_computation.28 | async-start | bytes 2359296 | tf_op jit(solution)/shard_map/all_gather | solution.py:262
  188.9 69.5 %all-to-all-start.1 = ((bf16[4,2,16384]{2,1,0:T(2,128)(2,1)}), bf16[4,2,16384]{2,1,0:T(2,128)(2,1)S(1)}, u32[]{:S(2)}, u32[]{:S(2)}) async-start(bf16[4,2,16384]{2,1,0:T(2,128)(2,1)} %reshape.455), calls=%async_computation.1 | async-start | bytes 524288 | tf_op jit(solution)/shard_map/all_to_all | solution.py:35
  193.5 217.8 %all-gather.27.cloned.1.call-start = ((), (), s32[]{:S(2)}) async-start(), calls=%async_computation.29 | async-start | bytes 4718592 | tf_op jit(solution)/shard_map/all_gather | solution.py:39
  289.8 25.9 %all-to-all-start.4 = ((bf16[4,2,16384]{2,1,0:T(2,128)(2,1)}), bf16[4,2,16384]{2,1,0:T(2,128)(2,1)S(1)}, u32[]{:S(2)}, u32[]{:S(2)}) async-start(bf16[4,2,16384]{2,1,0:T(2,128)(2,1)} %reshape.461), calls=%async_computation.4 | async-start | bytes 524288 | tf_op jit(solution)/shard_map/all_to_all | solution.py:35
  345.4 14.5 %all-to-all-start.5 = ((bf16[4,2,16384]{2,1,0:T(2,128)(2,1)}), bf16[4,2,16384]{2,1,0:T(2,128)(2,1)}, u32[]{:S(2)}, u32[]{:S(2)}) async-start(bf16[4,2,16384]{2,1,0:T(2,128)(2,1)} %reshape.463), calls=%async_computation.5 | async-start | bytes 524288 | tf_op jit(solution)/shard_map/all_to_all | solution.py:31
  383.4 97.7 %reduce-scatter.23.cloned.1.call-start = ((), (), s32[]{:S(2)}) async-start(), calls=%async_computation.31 | async-start | bytes 1179648 | tf_op jit(solution)/shard_map/reduce_scatter | solution.py:420
  403.7 231.7 %reduce-scatter.21.cloned.1.call-start = ((), (), s32[]{:S(2)}) async-start(), calls=%async_computation.30 | async-start | bytes 4718592 | tf_op jit(solution)/shard_map/reduce_scatter | solution.py:417
  481.0 203.9 %reduce-scatter.43.cloned.1.call-start = ((), (), s32[]{:S(2)}) async-start(), calls=%async_computation.41 | async-start | bytes 1179648
  494.0 218.4 %reduce-scatter.31.cloned.1.call-start = ((), (), s32[]{:S(2)}) async-start(), calls=%async_computation.35 | async-start | bytes 589824 | tf_op jit(solution)/shard_map/reduce_scatter | solution.py:469
  496.4 253.3 %reduce-scatter.29.cloned.1.call-start = ((), (), s32[]{:S(2)}) async-start(), calls=%async_computation.34 | async-start | bytes 589824 | tf_op jit(solution)/shard_map/reduce_scatter | solution.py:463
  498.7 288.9 %reduce-scatter.27.cloned.1.call-start = ((), (), s32[]{:S(2)}) async-start(), calls=%async_computation.33 | async-start | bytes 589824 | tf_op jit(solution)/shard_map/reduce_scatter | solution.py:460
  499.9 332.1 %reduce-scatter.33.cloned.1.call-start = ((), (), s32[]{:S(2)}) async-start(), calls=%async_computation.36 | async-start | bytes 2359296 | tf_op jit(solution)/shard_map/reduce_scatter | solution.py:472
  502.2 374.5 %reduce-scatter.35.cloned.1.call-start = ((), (), s32[]{:S(2)}) async-start(), calls=%async_computation.37 | async-start | bytes 2359296 | tf_op jit(solution)/shard_map/reduce_scatter | solution.py:478
  507.0 411.4 %reduce-scatter.25.cloned.1.call-start = ((), (), s32[]{:S(2)}) async-start(), calls=%async_computation.32 | async-start | bytes 1769472 | tf_op jit(solution)/shard_map/reduce_scatter | solution.py:457
  676.7 278.4 %reduce-scatter.41.cloned.1.call-start = ((), (), s32[]{:S(2)}) async-start(), calls=%async_computation.40 | async-start | bytes 147456
  682.7 309.7 %reduce-scatter.39.cloned.1.call-start = ((), (), s32[]{:S(2)}) async-start(), calls=%async_computation.39 | async-start | bytes 147456
  683.6 345.6 %reduce-scatter.37.cloned.1.call-start = ((), (), s32[]{:S(2)}) async-start(), calls=%async_computation.38 | async-start | bytes 147456
  684.8 407.4 %all-reduce.9.cloned.1.call-start = ((), (), s32[]{:S(2)}) async-start(), calls=%async_computation.42 | async-start | bytes 2359296 | tf_op jit(solution)/shard_map/psum | solution.py:506
  (83 other events, 3664.0 us)
Sparse Core Ops, SparseCore 0:
  9.9 28.8 all-gather.12
  40.7 23.4 all-gather.18
  77.3 26.0 all-gather.16
  105.7 27.8 all-gather.14
  136.0 23.4 all-gather.20
  161.3 27.9 all-gather.22
  191.1 27.8 all-gather.24
  221.0 56.2 all-gather.26
  387.4 45.4 reduce-scatter.22
  481.1 154.2 reduce-scatter.20
  638.9 36.0 reduce-scatter.42
  678.2 34.1 reduce-scatter.30
  715.5 34.0 reduce-scatter.28
  753.5 34.1 reduce-scatter.26
  790.8 41.1 reduce-scatter.32
  835.5 41.2 reduce-scatter.34
  879.9 38.4 reduce-scatter.24
  921.8 33.3 reduce-scatter.40
  959.1 33.3 reduce-scatter.38
  995.9 33.3 reduce-scatter.36
  1033.0 59.0 all-reduce.8
where the time goes:
time: 1120 us; the launch traced here: 1110 us
  waiting for transfers between devices  553 us (49%)
  blocking collectives  224 us (20%)
  local copies, waits for them, and re-layouts  111 us (10%)
  matrix products  99.9 us (9%)
  other arithmetic  52.8 us (5%)
  starting transfers between devices  25.5 us (2%)
  loops' own time  24.9 us (2%)
  between operations  19.4 us (2%)
    reduce_scatter x1, waiting for transfers between devices, shards(): lax.psum_scatter(self_terms.astype(jnp.bfloat16), 'shard', scatter_dimens...  128 us
    unnamed x25, waiting for transfers between devices  91.2 us
    all_gather x1, blocking collectives, shards(): lax.all_gather(self_out, 'shard', axis=0, tiled=True)  52.4 us
    reduce_scatter x1, waiting for transfers between devices, shards(): lax.psum_scatter(down_grad.astype(jnp.bfloat16), 'shard', scatter_dimensi...  44.8 us
    reduce_scatter x1, waiting for transfers between devices, shards(): lax.psum_scatter(up_grad.astype(jnp.bfloat16), 'shard', scatter_dimension...  44.3 us
    reduce_scatter x1, waiting for transfers between devices, shards(): lax.psum_scatter(proj_grad.astype(jnp.bfloat16), 'shard', scatter_dimensi...  41.6 us
    psum x1, waiting for transfers between devices, shards(): lax.psum(memory_part.astype(jnp.bfloat16), 'seq').astype(jnp.float32)  39.7 us
    all_to_all x2, blocking collectives, to_heads(): lax.all_to_all(stacked, 'seq', split_axis=1, concat_axis=2, tiled=True)  39.2 us
  transfers between devices with their start and end apart: 27, of which 17 were waited for; matrix products, arithmetic and copies ran while one was open for 22% of the time, Pallas kernels for 0%

commit v1 on v0

v1 whole, which is shorter than its diff:
```python
import functools

import jax
import jax.numpy as jnp
from jax import lax
from jax.experimental import pallas as pl
from jax.experimental.pallas import tpu as pltpu
from jax.sharding import PartitionSpec as P

H = 8
HD = 64
DOCS = 2
ENC = 1024
EPS = 1e-05
MASKED = -1e30
SCALE = HD**-0.5
MESH = pl.DeviceIdType.MESH
BF = jnp.bfloat16
F32 = jnp.float32
DMA = pltpu.SemaphoreType.DMA
ORDER = (0, 1, 2, 4, 3, 6, 5, 7)


def mm(a, b, ca=1, cb=0):
    return lax.dot_general(a, b, (((ca,), (cb,)), ((), ())), preferred_element_type=F32)


def flip(j, bits):
    low, mid, high = j % 2, (j // 2) % 2, (j // 4) % 2
    out = j
    if bits & 1:
        out = out + 1 - 2 * low
    if bits & 2:
        out = out + 2 - 4 * mid
    if bits & 4:
        out = out + 4 - 8 * high
    return out


def rcopy(src, dst, send_sem, recv_sem, device_id):
    return pltpu.make_async_remote_copy(
        src_ref=src,
        dst_ref=dst,
        send_sem=send_sem,
        recv_sem=recv_sem,
        device_id=device_id,
        device_id_type=MESH,
    )


def place():
    shard, seq = lax.axis_index("shard"), lax.axis_index("seq")
    return shard, seq, shard % 8, shard // 8


def greet(peers):
    barrier = pltpu.get_barrier_semaphore()
    count = 0
    for condition, device in peers:
        if condition is None:
            pl.semaphore_signal(barrier, inc=1, device_id=device, device_id_type=MESH)
            count = count + 1
        else:

            @pl.when(condition)
            def _(device=device):
                pl.semaphore_signal(barrier, inc=1, device_id=device, device_id_type=MESH)

            count = count + jnp.where(condition, 1, 0)
    pl.semaphore_wait(barrier, count)


def norm_stats(value):
    center = jnp.mean(value, axis=1, keepdims=True)
    offset = value - center
    spread = jnp.mean(offset * offset, axis=1, keepdims=True)
    scale = lax.rsqrt(spread + EPS)
    return offset * scale, scale


def norm_back(d_out, hat, scale, gain):
    d_hat = d_out * gain
    first = jnp.mean(d_hat, axis=1, keepdims=True)
    second = jnp.mean(d_hat * hat, axis=1, keepdims=True)
    d_in = scale * (d_hat - first - hat * second)
    return d_in, jnp.sum(d_out * hat, axis=0, keepdims=True), jnp.sum(d_out, axis=0, keepdims=True)


def embed(hid_ref, bound, vecs_ref, block):
    rows = hid_ref.shape[0]
    pos = block * rows + lax.broadcasted_iota(jnp.int32, (rows, 1), 0)
    picked = jnp.where(pos < bound, vecs_ref[0:1, :], vecs_ref[1:2, :])
    return hid_ref[...].astype(F32) + picked


def gather_kernel(
    S, Z, G, bnd, hid, small, wproj, wmem, enc, *rest
):
    W = 5
    weights = (wproj, wmem) + rest[:W]
    rest = rest[W:]
    x_all, kv, qt, mkv, enc_all, small_all, vecs = rest[:7]
    full = rest[7:14]
    (wsend, msend, w_all, m_all, sm_s, sm_r, w_s, w_r, mw_s, mw_r, x_s, x_r, e_s, e_r, z_s, z_r,
     mb_s, mb_r, g_s, g_f, g_r, l_s) = rest[14:]
    s, z, j, m = place()
    R = wproj.shape[0]
    T = hid.shape[0]
    bound = bnd[0]
    chips = S // 2
    core, chip = s % 2, s // 2
    sib = s + 1 - 2 * core

    greet(
        [(None, {"shard": (s + d) % S}) for d in range(1, S)]
        + [(z > 0, {"seq": z - 1}), (z < Z - 1, {"seq": z + 1})]
    )

    small_all[s] = small[...]
    small_copies = []
    for d in range(1, S):
        c = rcopy(small, small_all.at[s], sm_s.at[d], sm_r.at[s], {"shard": (s + d) % S})
        c.start()
        small_copies.append(c)
    for h in range(H):
        k = wproj[:, 512 + HD * h : 512 + HD * (h + 1)]
        v = wproj[:, 1024 + HD * h : 1024 + HD * (h + 1)]
        q = wproj[:, HD * h : HD * (h + 1)]
        wsend[h] = jnp.concatenate([k, v, q, jnp.zeros_like(q)], axis=1)
        msend[h] = jnp.concatenate(
            [wmem[:, HD * h : HD * (h + 1)], wmem[:, 512 + HD * h : 512 + HD * (h + 1)]], axis=1
        )
    w_all[s] = wsend[j]
    m_all[s] = msend[j]
    w_copies = []
    for d in range(1, S):
        p = (s + d) % S
        c = rcopy(wsend.at[p % 8], w_all.at[s], w_s.at[d], w_r.at[s], {"shard": p})
        c.start()
        w_copies.append(c)
        c = rcopy(msend.at[p % 8], m_all.at[s], mw_s.at[d], mw_r.at[s], {"shard": p})
        c.start()
        w_copies.append(c)
    for d in range(1, S):
        p = (s + d) % S
        rcopy(small, small_all.at[p], sm_s.at[d], sm_r.at[p], {"shard": p}).wait_recv()
    rows = jnp.zeros((16, 512), F32)
    for p in range(S):
        lane = lax.broadcasted_iota(jnp.int32, (256, 512), 0)
        col = lax.broadcasted_iota(jnp.int32, (256, 512), 1)
        pick = ((col - p * R) == lane) & (lane < R)
        rows = rows + mm(small_all[p], jnp.where(pick, 1.0, 0.0).astype(BF))
    vecs[...] = rows

    hat, _ = norm_stats(embed(hid, bound, vecs, s * Z + z))
    x_all[j] = (hat * vecs[2:3, :] + vecs[5:6, :]).astype(BF)
    enc_all[j] = enc[...]
    copies = []

    def send_block(ref, bits_source, bits_target, send, recv):
        source = flip(j, bits_source)
        c = rcopy(ref.at[source], ref.at[source], send, recv.at[source], {"shard": flip(s, bits_target)})
        c.start()
        copies.append(c)

    def wait_block(ref, bits, recv):
        source = flip(j, bits)
        rcopy(ref.at[source], ref.at[source], x_s.at[0], recv.at[source], {"shard": sib}).wait_recv()

    for n, bits in enumerate((1, 2, 4, 6)):
        send_block(x_all, 0, bits, x_s.at[n], x_r)
    for n, bits in enumerate((1, 2, 4, 6)):
        send_block(enc_all, 0, bits, e_s.at[n], e_r)
    for d in range(1, S):
        p = (s + d) % S
        rcopy(wsend.at[0], w_all.at[p], w_s.at[d], w_r.at[p], {"shard": p}).wait_recv()
        rcopy(msend.at[0], m_all.at[p], mw_s.at[d], mw_r.at[p], {"shard": p}).wait_recv()
    w_head = w_all[...].reshape(S * R, 256)
    m_head = m_all[...].reshape(S * R, 128)

    def z_copy(ref, block, plane, step, hop, slot):
        return rcopy(
            ref.at[:, block, plane] if block is not None else ref.at[:, :, plane],
            ref.at[:, block, plane] if block is not None else ref.at[:, :, plane],
            z_s.at[(step + 1) // 2, hop, slot],
            z_r.at[(step + 1) // 2, hop, slot],
            {"seq": z + step},
        )

    def z_send(ref, block, hop, slot):
        for step in (-1, 1):
            origin = z - step * hop
            ok = (z + step >= 0) & (z + step < Z) & (origin >= 0) & (origin < Z)

            @pl.when(ok)
            def _(step=step, origin=origin):
                z_copy(ref, block, origin, step, hop, slot).start()

    def z_recv(ref, block, hop, slot):
        for step in (-1, 1):
            origin = z - step * hop
            ok = (origin >= 0) & (origin < Z)

            @pl.when(ok)
            def _(step=step, origin=origin):
                z_copy(ref, block, origin, step, hop - 1, slot).wait_recv()

    def z_drain(ref, block, hop, slot):
        for step in (-1, 1):
            origin = z - step * hop
            ok = (z + step >= 0) & (z + step < Z) & (origin >= 0) & (origin < Z)

            @pl.when(ok)
            def _(step=step, origin=origin):
                z_copy(ref, block, origin, step, hop, slot).wait_send()

    def member_copy(ref, block, d, slot, mine):
        other = (m + d) % G
        at = m if mine else other
        view = ref.at[at, block, z] if block is not None else ref.at[at, :, z]
        return rcopy(view, view, mb_s.at[d, slot], mb_r.at[at, slot], {"shard": other * 8 + j})

    def spread(ref, block, slot):
        for d in range(1, G):
            member_copy(ref, block, d, slot, True).start()
        for d in range(1, G):
            member_copy(ref, block, d, slot, False).wait_recv()
        z_send(ref, block, 0, slot)

    for n, bits in enumerate(ORDER):
        block = flip(j, bits)
        if bits:
            wait_block(x_all, bits, x_r)
            if bits in (2, 4, 6):
                send_block(x_all, bits, 1, x_s.at[3 + bits // 2], x_r)
        kvq = mm(x_all[block], w_head)
        kv[m, block, z] = kvq[:, :128].astype(BF)
        spread(kv, block, n)
        qt[block] = (SCALE * kvq[:, 128:256].T[:HD]).astype(BF)

    for bits in (2, 4, 6):
        wait_block(enc_all, bits, e_r)
        send_block(enc_all, bits, 1, e_s.at[3 + bits // 2], e_r)
    for bits in (1, 3, 5, 7):
        wait_block(enc_all, bits, e_r)
    E = enc.shape[0]
    for b in range(8):
        mkv[m, b, z] = mm(enc_all[b], m_head).astype(BF)
    spread(mkv, None, 8)

    for a, (shard, whole) in enumerate(zip(weights, full)):
        pltpu.make_async_copy(shard, whole.at[s], l_s.at[a]).start()
        for d in range(1, chips):
            p = ((chip + d) % chips) * 2 + core
            rcopy(shard, whole.at[s], g_s.at[a, d], g_r.at[a, s], {"shard": p}).start()
        rcopy(shard, whole.at[s], g_s.at[a, 0], g_r.at[a, s], {"shard": sib}).start()

    for hop in range(1, Z):
        for n, bits in enumerate(ORDER):
            z_recv(kv, flip(j, bits), hop, n)
            z_send(kv, flip(j, bits), hop, n)
        z_recv(mkv, None, hop, 8)
        z_send(mkv, None, hop, 8)

    for a, (shard, whole) in enumerate(zip(weights, full)):
        for d in range(1, chips):
            q = ((chip + chips - d) % chips) * 2 + core
            rcopy(shard, whole.at[q], g_s.at[a, d], g_r.at[a, q], {"shard": sib}).wait_recv()
            rcopy(whole.at[q], whole.at[q], g_f.at[a, d], g_r.at[a, q], {"shard": sib}).start()
    for a, (shard, whole) in enumerate(zip(weights, full)):
        rcopy(shard, whole.at[sib], g_s.at[a, 0], g_r.at[a, sib], {"shard": sib}).wait_recv()
        for d in range(1, chips):
            q = ((chip + chips - d) % chips) * 2 + 1 - core
            rcopy(shard, whole.at[q], g_s.at[a, d], g_r.at[a, q], {"shard": sib}).wait_recv()
        pltpu.make_async_copy(shard, whole.at[s], l_s.at[a]).wait()
        for d in range(chips):
            rcopy(shard, whole.at[s], g_s.at[a, d], g_r.at[a, s], {"shard": sib}).wait_send()
        for d in range(1, chips):
            q = ((chip + chips - d) % chips) * 2 + core
            rcopy(whole.at[q], whole.at[q], g_f.at[a, d], g_r.at[a, q], {"shard": sib}).wait_send()
    for c in small_copies + w_copies + copies:
        c.wait_send()
    for n, bits in enumerate(ORDER):
        for d in range(1, G):
            member_copy(kv, flip(j, bits), d, n, True).wait_send()
        for hop in range(Z - 1):
            z_drain(kv, flip(j, bits), hop, n)
    for d in range(1, G):
        member_copy(mkv, None, d, 8, True).wait_send()
    for hop in range(Z - 1):
        z_drain(mkv, None, hop, 8)


def gather_call(S, Z, bnd, hid, small, wproj, wmem, enc, wout, wcq, wco, wup, wdn):
    G = S // 8
    T, R, E = hid.shape[0], wproj.shape[0], enc.shape[0]
    weights = (wproj, wmem, wout, wcq, wco, wup, wdn)
    vmem = pl.BlockSpec(memory_space=pltpu.VMEM)
    hbm = pl.BlockSpec(memory_space=pl.ANY)
    sds = jax.ShapeDtypeStruct
    outs = [
        sds((8, T, 512), BF),
        sds((G, 8, Z, T, 128), BF),
        sds((8, HD, T), BF),
        sds((G, 8, Z, E, 128), BF),
        sds((8, E, 512), BF),
        sds((S, 16, 256), BF),
        sds((16, 512), F32),
    ] + [sds((S,) + w.shape, BF) for w in weights]
    return pl.pallas_call(
        functools.partial(gather_kernel, S, Z, G),
        out_shape=outs,
        in_specs=[pl.BlockSpec(memory_space=pltpu.SMEM)] + [vmem] * 10,
        out_specs=[vmem] * 7 + [hbm] * 7,
        scratch_shapes=[
            pltpu.VMEM((8, R, 256), BF),
            pltpu.VMEM((8, R, 128), BF),
            pltpu.VMEM((S, R, 256), BF),
            pltpu.VMEM((S, R, 128), BF),
            DMA((S,)), DMA((S,)), DMA((S,)), DMA((S,)), DMA((S,)), DMA((S,)),
            DMA((8,)), DMA((8,)), DMA((8,)), DMA((8,)),
            DMA((2, Z, 9)), DMA((2, Z, 9)),
            DMA((G, 9)), DMA((G, 9)),
            DMA((7, S // 2)), DMA((7, S // 2)), DMA((7, S)), DMA((7,)),
        ],
        compiler_params=pltpu.CompilerParams(
            collective_id=0, has_side_effects=True, vmem_limit_bytes=60 << 20
        ),
        name="gather_qkv",
    )(bnd, hid, small, wproj, wmem, enc, wout, wcq, wco, wup, wdn)


def block_scores(kv_block, queries, key_first, bound, query_first, causal, masked):
    scores = mm(kv_block, queries)
    if not masked:
        return scores
    keys, count = kv_block.shape[0], queries.shape[1]
    query_pos = query_first + lax.broadcasted_iota(jnp.int32, (1, count), 1)
    key_pos = key_first + lax.broadcasted_iota(jnp.int32, (keys, 1), 0)
    if causal:
        least = jnp.where(query_pos < bound, 0, bound)
        allowed = (key_pos <= query_pos) & (key_pos >= least)
    else:
        allowed = jnp.where(query_pos < bound, 0, 1) == key_pos // ENC
    return jnp.where(allowed, scores, MASKED)


def attend_kernel(Z, causal, info, qt, kv, ot, of, lse, vt):
    bound, m, z = info[0], info[1], info[2]
    count, T = kv.shape[0], kv.shape[1]
    per_doc = ENC // T

    def first_block(pos):
        if causal:
            return jnp.where(pos < bound, 0, bound) // T
        return jnp.where(pos < bound, 0, per_doc)

    def last_block(block):
        if causal:
            return block
        return jnp.where(block * T + T - 1 < bound, per_doc, 2 * per_doc) - 1

    def turn_values(kb, carry):
        vt[kb] = kv[kb].astype(F32).T[HD:].astype(BF)
        return carry

    low = 8 * m * Z + z
    lax.fori_loop(first_block(low * T), last_block((8 * m + 7) * Z + z) + 1, turn_values, 0)

    def one_block(i, carry):
        bq = (8 * m + i) * Z + z
        q0 = bq * T
        queries = jnp.concatenate([qt[i], jnp.zeros((HD, T), BF)], axis=0)

        def step(masked, kb, state):
            top, total, acc = state
            scores = block_scores(kv[kb], queries, kb * T, bound, q0, causal, masked)
            new_top = jnp.maximum(top, jnp.max(scores, axis=0, keepdims=True))
            powers = jnp.exp(scores - new_top)
            fade = jnp.exp(top - new_top)
            total = total * fade + jnp.sum(powers, axis=0, keepdims=True)
            acc = acc * fade + mm(vt[kb], powers.astype(BF))
            return new_top, total, acc

        state = (
            jnp.full((1, T), MASKED, F32),
            jnp.zeros((1, T), F32),
            jnp.zeros((HD, T), F32),
        )
        begin, end = first_block(q0), last_block(bq) + 1
        if causal:
            tail = jnp.where(q0 + T - 1 < bound, 0, bound)
            plain = jnp.minimum(jnp.maximum((tail + T - 1) // T, begin), end - 1)
            state = lax.fori_loop(begin, plain, functools.partial(step, True), state)
            state = lax.fori_loop(plain, end - 1, functools.partial(step, False), state)
            state = step(True, end - 1, state)
        else:
            mixed = (q0 < bound) & (q0 + T - 1 >= bound)
            cut = jnp.where(mixed, end, begin)
            state = lax.fori_loop(begin, cut, functools.partial(step, True), state)
            state = lax.fori_loop(cut, end, functools.partial(step, False), state)
        top, total, acc = state
        result = acc / total
        ot[i] = result.astype(BF)
        of[i] = result
        lse[i] = top + jnp.log(total)
        return carry

    lax.fori_loop(0, 8, one_block, 0)


def attend(Z, causal, info, qt, kv):
    T = qt.shape[2]
    sds = jax.ShapeDtypeStruct
    vmem = pl.BlockSpec(memory_space=pltpu.VMEM)
    return pl.pallas_call(
        functools.partial(attend_kernel, Z, causal),
        out_shape=[sds((8, HD, T), BF), sds((8, HD, T), F32), sds((8, 1, T), F32)],
        in_specs=[pl.BlockSpec(memory_space=pltpu.SMEM), vmem, vmem],
        out_specs=[vmem] * 3,
        scratch_shapes=[pltpu.VMEM((kv.shape[0], HD, T), BF)],
        compiler_params=pltpu.CompilerParams(vmem_limit_bytes=60 << 20),
        name="attend_self" if causal else "attend_cross",
    )(info, qt, kv)


def attend_back_kernel(Z, causal, info, qt, kv, dt, of, lse, dq, dkv, qd, rows, delta, dqf):
    bound, m, z = info[0], info[1], info[2]
    count, T = kv.shape[0], kv.shape[1]
    per_doc = ENC // T

    def prepare(i, carry):
        zero = jnp.zeros((HD, T), BF)
        qd[i, :HD, :T] = qt[i]
        qd[i, HD:, :T] = zero
        qd[i, :HD, T:] = zero
        qd[i, HD:, T:] = dt[i]
        both = jnp.concatenate([qt[i].astype(F32), dt[i].astype(F32)], axis=0).T
        lane = lax.broadcasted_iota(jnp.int32, both.shape, 1)
        rows[i, :T] = jnp.where(lane < HD, 0.0, both).astype(BF)
        rows[i, T:] = jnp.where(lane < HD, both, 0.0).astype(BF)
        delta[i] = jnp.sum(dt[i].astype(F32) * of[i], axis=0, keepdims=True)
        dqf[i] = jnp.zeros((HD, T), F32)
        return carry

    lax.fori_loop(0, 8, prepare, 0)
    base = 8 * m * Z + z

    def clear(kb, carry):
        dkv[kb] = jnp.zeros(dkv.shape[1:], BF)
        return carry

    lax.fori_loop(0, count, clear, 0)

    def key_block(kb, carry):
        block = kv[kb]
        turned = block.astype(F32).T[:HD].astype(BF)
        k0 = kb * T

        def step(masked, i, acc):
            q0 = (base + i * Z) * T
            both = mm(block, qd[i])
            scores, d_probs = both[:, :T], both[:, T:]
            if masked:
                query_pos = q0 + lax.broadcasted_iota(jnp.int32, (1, T), 1)
                key_pos = k0 + lax.broadcasted_iota(jnp.int32, (T, 1), 0)
                if causal:
                    least = jnp.where(query_pos < bound, 0, bound)
                    allowed = (key_pos <= query_pos) & (key_pos >= least)
                else:
                    allowed = jnp.where(query_pos < bound, 0, 1) == key_pos // ENC
                scores = jnp.where(allowed, scores, MASKED)
            probs = jnp.exp(scores - lse[i])
            d_raw = (probs * (d_probs - delta[i])).astype(BF)
            dqf[i] += mm(turned, d_raw)
            return acc + mm(jnp.concatenate([probs.astype(BF), d_raw], axis=1), rows[i])

        def chosen(i, acc):
            q0 = (base + i * Z) * T
            if causal:
                tail = jnp.where(q0 + T - 1 < bound, 0, bound)
                masked = (base + i * Z == kb) | (k0 < tail)
            else:
                masked = (q0 < bound) & (q0 + T - 1 >= bound)
            return lax.cond(
                masked, functools.partial(step, True), functools.partial(step, False), i, acc
            )

        if causal:
            begin = jnp.maximum(kb - base + Z - 1, 0) // Z
            reach = jnp.minimum(8, jnp.maximum((bound + T - 1) // T - base + Z - 1, 0) // Z)
            end = jnp.where(k0 + T - 1 < bound, reach, 8)
        else:
            firsts = jnp.minimum(8, jnp.maximum((bound + T - 1) // T - base + Z - 1, 0) // Z)
            wholes = jnp.minimum(8, jnp.maximum(bound // T - base + Z - 1, 0) // Z)
            begin = jnp.where(kb < per_doc, 0, wholes)
            end = jnp.where(kb < per_doc, firsts, 8)
        acc = lax.fori_loop(begin, end, chosen, jnp.zeros((T, 128), F32))
        dkv[kb] = acc.astype(BF)
        return carry

    if causal:
        start = jnp.where(base * T < bound, 0, bound) // T
        lax.fori_loop(start, base + 7 * Z + 1, key_block, 0)
    else:
        lax.fori_loop(0, count, key_block, 0)

    def finish(i, carry):
        dq[i] = (SCALE * dqf[i]).astype(BF)
        return carry

    lax.fori_loop(0, 8, finish, 0)


def attend_back(Z, causal, info, qt, kv, dt, of, lse):
    T = qt.shape[2]
    sds = jax.ShapeDtypeStruct
    vmem = pl.BlockSpec(memory_space=pltpu.VMEM)
    return pl.pallas_call(
        functools.partial(attend_back_kernel, Z, causal),
        out_shape=[sds((8, HD, T), BF), sds(kv.shape, BF)],
        in_specs=[pl.BlockSpec(memory_space=pltpu.SMEM)] + [vmem] * 5,
        out_specs=[vmem] * 2,
        scratch_shapes=[
            pltpu.VMEM((8, 128, 2 * T), BF),
            pltpu.VMEM((8, 2 * T, 128), BF),
            pltpu.VMEM((8, 1, T), F32),
            pltpu.VMEM((8, HD, T), F32),
        ],
        compiler_params=pltpu.CompilerParams(vmem_limit_bytes=60 << 20),
        name="attend_self_back" if causal else "attend_cross_back",
    )(info, qt, kv, dt, of, lse)


def greet_group():
    s, z, j, m = place()
    greet([(None, {"shard": m * 8 + (j + d) % 8}) for d in range(1, 8)])


def exchange_copies(src, dst, send, recv):
    s, z, j, m = place()
    out = []
    for d in (1, 2, 3, 4, 5, 6, 7):
        p = flip(j, d)
        out.append(rcopy(src.at[p], dst.at[j], send.at[d], recv.at[j], {"shard": m * 8 + p}))
    return out


def exchange_start(src, dst, send, recv):
    s, z, j, m = place()
    for c in exchange_copies(src, dst, send, recv):
        c.start()
    dst[j] = src[j]


def exchange_recv(src, dst, send, recv):
    s, z, j, m = place()
    for d in (1, 2, 3, 4, 5, 6, 7):
        p = flip(j, d)
        rcopy(src.at[p], dst.at[p], send.at[d], recv.at[p], {"shard": m * 8 + p}).wait_recv()


def exchange_sent(src, dst, send, recv):
    for c in exchange_copies(src, dst, send, recv):
        c.wait_send()


def remote_call(kernel, name, ident, ins, outs, scratch, smem=1, far=()):
    vmem = pl.BlockSpec(memory_space=pltpu.VMEM)
    in_specs = [pl.BlockSpec(memory_space=pltpu.SMEM)] * smem + [vmem] * (len(ins) - smem)
    for n in far:
        in_specs[n] = pl.BlockSpec(memory_space=pl.ANY)
    return pl.pallas_call(
        kernel,
        out_shape=outs,
        in_specs=in_specs,
        out_specs=[vmem] * len(outs),
        scratch_shapes=scratch,
        compiler_params=pltpu.CompilerParams(
            collective_id=ident, has_side_effects=True, vmem_limit_bytes=60 << 20
        ),
        name=name,
    )(*ins)


def middle_kernel(Z, bnd, ot, hid, vecs, wout, wcq, at, after, n2, cqt, cq_send, s1, r1, s2, r2):
    s, z, j, m = place()
    T = hid.shape[0]
    greet_group()
    exchange_start(ot, at, s1, r1)
    base = embed(hid, bnd[0], vecs, s * Z + z)
    exchange_recv(ot, at, s1, r1)
    attn = at[...].reshape(512, T).astype(F32).T.astype(BF)
    value = base + mm(attn, wout[...])
    after[...] = value
    hat, _ = norm_stats(value)
    normed = (hat * vecs[3:4, :] + vecs[6:7, :]).astype(BF)
    n2[...] = normed
    cq = mm(normed, wcq[...])
    cq_send[...] = (SCALE * cq.T).astype(BF).reshape(8, HD, T)
    exchange_start(cq_send, cqt, s2, r2)
    exchange_recv(cq_send, cqt, s2, r2)
    exchange_sent(ot, at, s1, r1)
    exchange_sent(cq_send, cqt, s2, r2)


def middle(Z, bnd, ot, hid, vecs, wout, wcq):
    T = hid.shape[0]
    sds = jax.ShapeDtypeStruct
    return remote_call(
        functools.partial(middle_kernel, Z),
        "middle",
        1,
        (bnd, ot, hid, vecs, wout, wcq),
        [sds((8, HD, T), BF), sds((T, 512), F32), sds((T, 512), BF), sds((8, HD, T), BF)],
        [pltpu.VMEM((8, HD, T), BF), DMA((8,)), DMA((8,)), DMA((8,)), DMA((8,))],
    )


def erf(x):
    return lax.erf(x)


def feed_kernel(
    crt, after, vecs, upb, wco, wup, wdn, grad,
    layer_out, d_after, co_grad, up_grad, dn_grad, smalls, upb_grad, dct,
    ct, send, n3t, out_acc, dn_acc, s1, r1, s2, r2,
):
    T = after.shape[0]
    FF = wup.shape[1]
    greet_group()
    exchange_start(crt, ct, s1, r1)
    g = grad[...]
    gf = g.astype(F32)
    gt = gf.T.astype(BF)
    exchange_recv(crt, ct, s1, r1)
    cross_t = ct[...].reshape(512, T)
    value = after[...] + mm(cross_t.astype(F32).T.astype(BF), wco[...])
    hat, scale = norm_stats(value)
    normed = hat * vecs[4:5, :] + vecs[7:8, :]
    n3 = normed.astype(BF)
    n3t[...] = n3.astype(F32).T.astype(BF)
    out_acc[...] = value + vecs[9:10, :]
    dn_acc[...] = jnp.zeros_like(dn_acc)
    width = 512
    for c in range(FF // width):
        lo, hi = c * width, (c + 1) * width
        pre = mm(n3, wup[:, lo:hi]) + upb[0:1, lo:hi].astype(F32)
        half = 0.5 * (1.0 + erf(pre * (0.5**0.5)))
        middle_c = (pre * half).astype(BF)
        out_acc[...] += mm(middle_c, wdn[lo:hi, :])
        slope = half + pre * (jnp.exp(-0.5 * pre * pre) * ((0.5 / jnp.pi) ** 0.5))
        d_pre = mm(g, wdn[lo:hi, :], 1, 1) * slope
        d_pre_b = d_pre.astype(BF)
        upb_grad[0:1, lo:hi] = jnp.sum(d_pre_b.astype(F32), axis=0, keepdims=True)
        dn_grad[lo:hi, :] = mm(middle_c.astype(F32).T.astype(BF), g).astype(BF)
        up_grad[:, lo:hi] = mm(n3t[...], d_pre_b).astype(BF)
        dn_acc[...] += mm(d_pre_b, wup[:, lo:hi], 1, 1)
    layer_out[...] = out_acc[...].astype(BF)
    d_value, d_gain, d_shift = norm_back(dn_acc[...], hat, scale, vecs[4:5, :])
    total = gf + d_value
    d_after[...] = total
    smalls[0:1, :] = d_gain
    smalls[1:2, :] = d_shift
    smalls[2:3, :] = jnp.sum(gf, axis=0, keepdims=True)
    dc = total.astype(BF)
    d_cross = mm(wco[...], dc, 1, 1)
    send[...] = d_cross.astype(BF).reshape(8, HD, T)
    exchange_start(send, dct, s2, r2)
    co_grad[...] = mm(cross_t, dc).astype(BF)
    exchange_recv(send, dct, s2, r2)
    exchange_sent(crt, ct, s1, r1)
    exchange_sent(send, dct, s2, r2)


def feed(crt, after, vecs, upb, wco, wup, wdn, grad):
    T, FF = after.shape[0], wup.shape[1]
    sds = jax.ShapeDtypeStruct
    return remote_call(
        feed_kernel,
        "feed_forward",
        2,
        (crt, after, vecs, upb, wco, wup, wdn, grad),
        [
            sds((T, 512), BF),
            sds((T, 512), F32),
            sds((512, 512), BF),
            sds((512, FF), BF),
            sds((FF, 512), BF),
            sds((8, 512), F32),
            sds((1, FF), F32),
            sds((8, HD, T), BF),
        ],
        [
            pltpu.VMEM((8, HD, T), BF),
            pltpu.VMEM((8, HD, T), BF),
            pltpu.VMEM((512, T), BF),
            pltpu.VMEM((T, 512), F32),
            pltpu.VMEM((T, 512), F32),
            DMA((8,)), DMA((8,)), DMA((8,)), DMA((8,)),
        ],
        smem=0,
    )


def middle_back_kernel(
    dcqt, after, d_after2, n2, at, vecs, wcq, wout,
    d_after, cq_grad, out_grad, smalls, dat,
    home, send, s1, r1, s2, r2,
):
    T = after.shape[0]
    greet_group()
    exchange_start(dcqt, home, s1, r1)
    hat, scale = norm_stats(after[...])
    n2t = n2[...].astype(F32).T.astype(BF)
    exchange_recv(dcqt, home, s1, r1)
    dcq = home[...].reshape(512, T).astype(F32).T.astype(BF)
    d_value, d_gain, d_shift = norm_back(mm(dcq, wcq[...], 1, 1), hat, scale, vecs[3:4, :])
    total = d_after2[...] + d_value
    d_after[...] = total
    smalls[0:1, :] = d_gain
    smalls[1:2, :] = d_shift
    da = total.astype(BF)
    send[...] = mm(wout[...], da, 1, 1).astype(BF).reshape(8, HD, T)
    exchange_start(send, dat, s2, r2)
    cq_grad[...] = mm(n2t, dcq).astype(BF)
    out_grad[...] = mm(at[...].reshape(512, T), da).astype(BF)
    exchange_recv(send, dat, s2, r2)
    exchange_sent(dcqt, home, s1, r1)
    exchange_sent(send, dat, s2, r2)


def middle_back(dcqt, after, d_after2, n2, at, vecs, wcq, wout):
    T = after.shape[0]
    sds = jax.ShapeDtypeStruct
    return remote_call(
        middle_back_kernel,
        "middle_back",
        3,
        (dcqt, after, d_after2, n2, at, vecs, wcq, wout),
        [
            sds((T, 512), F32),
            sds((512, 512), BF),
            sds((512, 512), BF),
            sds((8, 512), F32),
            sds((8, HD, T), BF),
        ],
        [
            pltpu.VMEM((8, HD, T), BF),
            pltpu.VMEM((8, HD, T), BF),
            DMA((8,)), DMA((8,)), DMA((8,)), DMA((8,)),
        ],
        smem=0,
    )


NC = 16


def last_kernel(
    S, Z, G,
    info, hid, vecs, d_after, x_all, enc_all, dqt, dkv, dmkv, wproj, wmem,
    out_g, cq_g, co_g, up_g, dn_g, smalls_in,
    hidden_grad, encoder_grad, proj_o, out_o, cq_o, mem_o, co_o, up_o, dn_o, smalls_o,
    sib_out, sib_cq, sib_co, sib_up, sib_dn, got_out, got_cq, got_co, got_up, got_dn,
    rk, rm, fin, finm, mbuf, mbufm, hkv, hq, hm, dall, psend, pgot, msend, mgot,
    wz, zin, zfin, sm_all, sm_z, sm_plane, sm_mine,
    a_s, a_r, b_s, b_r, k_s, k_r, mb_s, mb_r, hq_s, hq_r, hk_s, hk_r, hm_s, hm_r,
    p_s, p_r, pm_s, pm_r, c_s, c_r, f_s, f_r, sm_s, sm_r, sz_s, sz_r,
):
    s, z, j, m = place()
    T, E = hid.shape[0], enc_all.shape[1]
    R = 512 // S
    F = dn_g.shape[0] // S
    bound = info[0]
    chips = S // 2
    core, chip = s % 2, s // 2
    sib = s + 1 - 2 * core
    greet(
        [(None, {"shard": (s + d) % S}) for d in range(1, S)]
        + [(None, {"seq": (z + d) % Z}) for d in range(1, Z)]
    )
    grads = ((out_g, R), (cq_g, R), (co_g, R), (up_g, R), (dn_g, F))
    sibs = (sib_out, sib_cq, sib_co, sib_up, sib_dn)
    gots = (got_out, got_cq, got_co, got_up, got_dn)

    def piece(a, p):
        ref, rows = grads[a]
        return ref.at[pl.ds(pl.multiple_of(p * rows, rows), rows), :]

    def sib_copy(a, q):
        return rcopy(piece(a, 2 * q + 1 - core), sibs[a].at[q], a_s.at[a, q], a_r.at[a, q], {"shard": sib})

    for q in range(chips):
        for a in range(5):
            sib_copy(a, q).start()
    exchange_start(dqt, hq, hq_s, hq_r)

    if G > 1:
        for d in range(1, G):
            o = (m + d) % G
            rcopy(dkv.at[o], mbuf.at[m], mb_s.at[d, 0], mb_r.at[m, 0], {"shard": o * 8 + j}).start()
            rcopy(dmkv.at[o], mbufm.at[m], mb_s.at[d, 1], mb_r.at[m, 1], {"shard": o * 8 + j}).start()
        own_part = pltpu.make_async_copy(dkv.at[m], mbuf.at[m], mb_s.at[0, 0])
        own_part.start()
        own_part.wait()
        for d in range(1, G):
            o = (m + d) % G
            rcopy(dkv.at[o], mbuf.at[o], mb_s.at[d, 0], mb_r.at[o, 0], {"shard": o * 8 + j}).wait_recv()
            rcopy(dmkv.at[o], mbufm.at[o], mb_s.at[d, 1], mb_r.at[o, 1], {"shard": o * 8 + j}).wait_recv()
        for b in range(8):
            acc = mbuf[m, b].astype(F32)
            accm = dmkv[m, b].astype(F32)
            for d in range(1, G):
                acc = acc + mbuf[(m + d) % G, b].astype(F32)
                accm = accm + mbufm[(m + d) % G, b].astype(F32)
            mbuf[m, b] = acc.astype(BF)
            mbufm[m, b] = accm.astype(BF)
        part, partm = mbuf.at[m], mbufm.at[m]
    else:
        part, partm = dkv.at[0], dmkv.at[0]

    def z_view(slot, t):
        return part.at[slot, t] if slot < 8 else partm.at[:, t]

    def z_buffer(way, t, slot):
        return rk.at[way, t, slot] if slot < 8 else rm.at[way, t]

    def z_copy(way, t, slot, source):
        step = 2 * way - 1
        return rcopy(
            source, z_buffer(way, t, slot), k_s.at[way, t, slot], k_r.at[way, t, slot], {"seq": z + step}
        )

    ends = (Z - 1, 0)
    for far in range(Z - 1, 0, -1):
        for slot in range(9):
            for way in (0, 1):
                t = z + (2 * way - 1) * far

                @pl.when((z == ends[way]) & (t >= 0) & (t < Z))
                def _(way=way, t=t, slot=slot):
                    z_copy(way, t, slot, z_view(slot, t)).start()

    def own_copy(a, q):
        return rcopy(
            sibs[a].at[q], gots[a].at[chip], b_s.at[a, q], b_r.at[a, chip], {"shard": 2 * q + core}
        )

    for d in range(chips):
        q = (chip + d + 1) % chips
        for a in range(5):
            sib_copy(a, q).wait_recv()
            sibs[a][q] = (
                sibs[a][q].astype(F32) + piece(a, 2 * q + core)[...].astype(F32)
            ).astype(BF)
            if d < chips - 1:
                own_copy(a, q).start()

    turned = x_all[...].reshape(8 * T, 512).astype(F32).T.astype(BF)
    for b in range(8):
        dq_b = dqt[b].astype(F32)
        dall[b * T : (b + 1) * T, 128:] = jnp.concatenate([dq_b, jnp.zeros_like(dq_b)], axis=0).T.astype(BF)

    for far in range(Z - 1, 0, -1):
        for slot in range(9):
            for way in (0, 1):
                t = z + (2 * way - 1) * far

                @pl.when((z != ends[way]) & (t >= 0) & (t < Z))
                def _(way=way, t=t, slot=slot):
                    z_copy(way, t, slot, z_view(slot, t)).wait_recv()
                    buf = z_buffer(way, t, slot)
                    buf[...] = (
                        buf[...].astype(F32) + z_view(slot, t)[...].astype(F32)
                    ).astype(BF)
                    z_copy(way, t, slot, buf).start()

    for slot in range(9):
        for way in (0, 1):

            @pl.when(z != ends[way])
            def _(way=way, slot=slot):
                z_copy(way, z, slot, z_view(slot, z)).wait_recv()

        low = jnp.where(z == ends[0], 0.0, z_buffer(0, z, slot)[...].astype(F32))
        high = jnp.where(z == ends[1], 0.0, z_buffer(1, z, slot)[...].astype(F32))
        total = (low + high + z_view(slot, z)[...].astype(F32)).astype(BF)
        if slot < 8:
            fin[slot] = total
        else:
            finm[...] = total

    mine, minem = fin, finm
    exchange_start(mine, hkv, hk_s, hk_r)
    exchange_start(minem, hm, hm_s, hm_r)

    for b in range(8):
        dall[b * T : (b + 1) * T, :128] = mine[b]
    psend[...] = mm(turned, dall[...]).astype(BF).reshape(S, R, 256)
    enc_turned = enc_all[...].reshape(8 * E, 512).astype(F32).T.astype(BF)
    msend[...] = mm(enc_turned, minem[...].reshape(8 * E, 128)).astype(BF).reshape(S, R, 128)
    pgot[s] = psend[s]
    mgot[s] = msend[s]
    for d in range(1, S):
        p = (s + d) % S
        rcopy(psend.at[p], pgot.at[s], p_s.at[d], p_r.at[s], {"shard": p}).start()
        rcopy(msend.at[p], mgot.at[s], pm_s.at[d], pm_r.at[s], {"shard": p}).start()

    for a in range(5):
        for d in range(1, chips):
            q = (chip + d) % chips
            rcopy(sibs[a].at[q], gots[a].at[q], b_s.at[a, q], b_r.at[a, q], {"shard": 2 * q + core}).wait_recv()
        total = sibs[a][chip].astype(F32)
        for d in range(1, chips):
            total = total + gots[a][(chip + d) % chips].astype(F32)
        total = total.astype(BF)
        if a < 3:
            wz[a] = total
        elif a == 3:
            for c in range(4):
                wz[3 + c] = total[:, 512 * c : 512 * (c + 1)]
        else:
            for c in range(4):
                wz[7 + c] = total[c * R : (c + 1) * R]

    block = s * Z + z
    value = embed(hid, bound, vecs, block)
    hat, scale = norm_stats(value)
    exchange_recv(dqt, hq, hq_s, hq_r)
    exchange_recv(mine, hkv, hk_s, hk_r)
    exchange_recv(minem, hm, hm_s, hm_r)
    d_query = hq[...].reshape(512, T).astype(F32).T.astype(BF)
    d_keys = jnp.concatenate([hkv[h][:, :HD] for h in range(H)], axis=1)
    d_values = jnp.concatenate([hkv[h][:, HD:] for h in range(H)], axis=1)
    d_norm = (
        mm(d_query, wproj[:, :512], 1, 1)
        + mm(d_keys, wproj[:, 512:1024], 1, 1)
        + mm(d_values, wproj[:, 1024:], 1, 1)
    )
    d_value, d_gain, d_shift = norm_back(d_norm, hat, scale, vecs[2:3, :])
    total = d_after[...] + d_value
    hidden_grad[...] = total
    pos = block * T + lax.broadcasted_iota(jnp.int32, (T, 1), 0)
    first = jnp.sum(jnp.where(pos < bound, total, 0.0), axis=0, keepdims=True)
    second = jnp.sum(jnp.where(pos < bound, 0.0, total), axis=0, keepdims=True)
    sm_mine[...] = smalls_in[...]
    sm_mine[0:1, :] = d_gain
    sm_mine[3:4, :] = d_shift
    sm_mine[6:7, :] = first
    sm_mine[7:8, :] = second
    for d in range(1, S):
        rcopy(sm_mine, sm_all.at[s], sm_s.at[d], sm_r.at[s], {"shard": (s + d) % S}).start()
    sm_all[s] = sm_mine[...]
    e_keys = jnp.concatenate([hm[h][:, :HD] for h in range(H)], axis=1)
    e_values = jnp.concatenate([hm[h][:, HD:] for h in range(H)], axis=1)
    encoder_grad[...] = mm(e_keys, wmem[:, :512], 1, 1) + mm(e_values, wmem[:, 512:], 1, 1)

    for d in range(1, S):
        p = (s + d) % S
        rcopy(psend.at[p], pgot.at[p], p_s.at[d], p_r.at[p], {"shard": p}).wait_recv()
        rcopy(msend.at[p], mgot.at[p], pm_s.at[d], pm_r.at[p], {"shard": p}).wait_recv()
    heads, mheads = [], []
    for h in range(H):
        acc, accm = pgot[h].astype(F32), mgot[h].astype(F32)
        for g in range(1, G):
            acc = acc + pgot[8 * g + h].astype(F32)
            accm = accm + mgot[8 * g + h].astype(F32)
        heads.append(acc)
        mheads.append(accm)
    wz[11] = jnp.concatenate([v[:, 128 : 128 + HD] for v in heads], axis=1).astype(BF)
    wz[12] = jnp.concatenate([v[:, :HD] for v in heads], axis=1).astype(BF)
    wz[13] = jnp.concatenate([v[:, HD:128] for v in heads], axis=1).astype(BF)
    wz[14] = jnp.concatenate([v[:, :HD] for v in mheads], axis=1).astype(BF)
    wz[15] = jnp.concatenate([v[:, HD:] for v in mheads], axis=1).astype(BF)

    def inward(k, step):
        way = (step + 1) // 2
        return rcopy(wz.at[k], zin.at[way, k], c_s.at[way, k], c_r.at[way, k], {"seq": z + step})

    def outward(k, step):
        return rcopy(zfin.at[k], zfin.at[k], f_s.at[(step + 1) // 2, k], f_r.at[k], {"seq": z + step})

    def reduce_in(k, r):
        for step, beyond in ((-1, z > r), (1, z < r)):
            tip = ends[0] if step < 0 else ends[1]
            way = (step + 1) // 2

            @pl.when(beyond)
            def _(step=step, tip=tip, way=way):
                @pl.when(z != tip)
                def _():
                    inward(k, step).wait_recv()
                    wz[k] = (wz[k].astype(F32) + zin[way, k].astype(F32)).astype(BF)

                inward(k, step).start()

        @pl.when(z == r)
        def _():
            total = wz[k].astype(F32)
            if r < Z - 1:
                inward(k, -1).wait_recv()
                total = total + zin[0, k].astype(F32)
            if r > 0:
                inward(k, 1).wait_recv()
                total = total + zin[1, k].astype(F32)
            zfin[k] = total.astype(BF)
            if r < Z - 1:
                outward(k, 1).start()
            if r > 0:
                outward(k, -1).start()

    def send_out(k, r):
        for step, beyond in ((1, z > r), (-1, z < r)):
            tip = Z - 1 if step > 0 else 0

            @pl.when(beyond)
            def _(step=step, tip=tip):
                outward(k, step).wait_recv()

                @pl.when(z != tip)
                def _():
                    outward(k, step).start()

        value = zfin[k].astype(F32)
        if k == 0:
            out_o[...] = value
        elif k == 1:
            cq_o[...] = value
        elif k == 2:
            co_o[...] = value
        elif k < 7:
            up_o[:, 512 * (k - 3) : 512 * (k - 2)] = value
        elif k < 11:
            dn_o[(k - 7) * R : (k - 6) * R, :] = value
        elif k < 14:
            proj_o[:, 512 * (k - 11) : 512 * (k - 10)] = value
        else:
            mem_o[:, 512 * (k - 14) : 512 * (k - 13)] = value

    def root(k):
        return max(Z // 2 - 1 + k % 2, 0) if Z > 1 else 0

    lag = 3
    for k in range(NC + lag):
        if k < NC:
            reduce_in(k, root(k))
        if k >= lag:
            send_out(k - lag, root(k - lag))
        if k == 4:
            for d in range(1, S):
                p = (s + d) % S
                rcopy(sm_mine, sm_all.at[p], sm_s.at[d], sm_r.at[p], {"shard": p}).wait_recv()
            acc = sm_all[0]
            for p in range(1, S):
                acc = acc + sm_all[p]
            sm_plane[...] = acc
            for d in range(1, Z):
                rcopy(sm_plane, sm_z.at[z], sz_s.at[d], sz_r.at[z], {"seq": (z + d) % Z}).start()
            sm_z[z] = acc
    for d in range(1, Z):
        o = (z + d) % Z
        rcopy(sm_plane, sm_z.at[o], sz_s.at[d], sz_r.at[o], {"seq": o}).wait_recv()
    acc = sm_z[0]
    for o in range(1, Z):
        acc = acc + sm_z[o]
    smalls_o[...] = acc

    for a in range(5):
        for q in range(chips):
            sib_copy(a, q).wait_send()
        for d in range(1, chips):
            own_copy(a, (chip + d) % chips).wait_send()
    for d in range(1, G):
        o = (m + d) % G
        rcopy(dkv.at[o], mbuf.at[m], mb_s.at[d, 0], mb_r.at[m, 0], {"shard": o * 8 + j}).wait_send()
        rcopy(dmkv.at[o], mbufm.at[m], mb_s.at[d, 1], mb_r.at[m, 1], {"shard": o * 8 + j}).wait_send()
    exchange_sent(dqt, hq, hq_s, hq_r)
    exchange_sent(mine, hkv, hk_s, hk_r)
    exchange_sent(minem, hm, hm_s, hm_r)
    for far in range(Z - 1, 0, -1):
        for slot in range(9):
            for way in (0, 1):
                t = z + (2 * way - 1) * far

                @pl.when((t >= 0) & (t < Z))
                def _(way=way, t=t, slot=slot):
                    z_copy(way, t, slot, z_view(slot, t)).wait_send()

    for d in range(1, S):
        p = (s + d) % S
        rcopy(psend.at[p], pgot.at[s], p_s.at[d], p_r.at[s], {"shard": p}).wait_send()
        rcopy(msend.at[p], mgot.at[s], pm_s.at[d], pm_r.at[s], {"shard": p}).wait_send()
        rcopy(sm_mine, sm_all.at[s], sm_s.at[d], sm_r.at[s], {"shard": p}).wait_send()
    for d in range(1, Z):
        rcopy(sm_plane, sm_z.at[z], sz_s.at[d], sz_r.at[z], {"seq": (z + d) % Z}).wait_send()
    for k in range(NC):
        r = root(k)
        for step, beyond in ((-1, z > r), (1, z < r)):

            @pl.when(beyond)
            def _(step=step):
                inward(k, step).wait_send()

        for step in (-1, 1):
            sends = (z >= r) & (z < Z - 1) if step > 0 else (z <= r) & (z > 0)

            @pl.when(sends)
            def _(step=step):
                outward(k, step).wait_send()


def last(v):
    S, Z, G = v["S"], v["Z"], v["G"]
    T, R, F, E = v["T"], v["R"], v["F"], v["encoder"].shape[0]
    s = v["s"]
    FF = v["wup"].shape[1]
    chips = S // 2
    smalls = jnp.concatenate(
        [
            jnp.zeros((1, 512), F32), v["small2"][0:1], v["small3"][0:1],
            jnp.zeros((1, 512), F32), v["small2"][1:2], v["small3"][1:2],
            jnp.zeros((2, 512), F32), v["small3"][2:3], v["upb_grad"].reshape(FF // 512, 512),
            jnp.zeros((7 - FF // 512, 512), F32),
        ],
        axis=0,
    )
    sds = jax.ShapeDtypeStruct
    V = pltpu.VMEM
    res = remote_call(
        functools.partial(last_kernel, S, Z, G),
        "gradients_home",
        4,
        (
            v["info"], v["hidden_in"], v["vecs"], v["d_after"], v["x_all"], v["enc_all"], v["dqt"],
            v["dkv"].reshape(G, 8, Z, T, 128), v["dmkv"].reshape(G, 8, Z, E, 128), v["wproj"], v["wmem"],
            v["wout_grad"], v["cq_grad"], v["co_grad"], v["up_grad"], v["dn_grad"], smalls,
        ),
        [
            sds((T, 512), F32), sds((E, 512), F32), sds((R, 1536), F32), sds((R, 512), F32),
            sds((R, 512), F32), sds((R, 1024), F32), sds((R, 512), F32), sds((R, FF), F32),
            sds((F, 512), F32), sds((16, 512), F32),
        ],
        [V((chips, R, 512), BF)] * 3 + [V((chips, R, FF), BF), V((chips, F, 512), BF)]
        + [V((chips, R, 512), BF)] * 3 + [V((chips, R, FF), BF), V((chips, F, 512), BF)]
        + [
            V((2, Z, 8, T, 128), BF), V((2, Z, 8, E, 128), BF),
            V((8, T, 128), BF), V((8, E, 128), BF),
            V((G if G > 1 else 1, 8, Z if G > 1 else 1, T, 128), BF),
            V((G if G > 1 else 1, 8, Z if G > 1 else 1, E, 128), BF),
            V((8, T, 128), BF), V((8, HD, T), BF), V((8, E, 128), BF),
            V((8 * T, 256), BF),
            V((S, R, 256), BF), V((S, R, 256), BF), V((S, R, 128), BF), V((S, R, 128), BF),
            V((NC, R, 512), BF), V((2, NC, R, 512), BF), V((NC, R, 512), BF),
            V((S, 16, 512), F32), V((Z, 16, 512), F32), V((16, 512), F32), V((16, 512), F32),
            DMA((5, chips)), DMA((5, chips)), DMA((5, chips)), DMA((5, chips)),
            DMA((2, Z, 9)), DMA((2, Z, 9)), DMA((G, 2)), DMA((G, 2)),
            DMA((8,)), DMA((8,)), DMA((8,)), DMA((8,)), DMA((8,)), DMA((8,)),
            DMA((S,)), DMA((S,)), DMA((S,)), DMA((S,)),
            DMA((2, NC)), DMA((2, NC)), DMA((2, NC)), DMA((NC,)),
            DMA((S,)), DMA((S,)), DMA((Z,)), DMA((Z,)),
        ],
        far=(7,) if G > 1 else (),
    )
    hidden_grad, encoder_grad, proj_o, out_o, cq_o, mem_o, co_o, up_o, dn_o, sums = res

    def own(rows, width):
        return lax.dynamic_slice(rows, (0, s * width), (rows.shape[0], width))

    step_hot = v["step_hot"].astype(F32)
    time_rows = own(sums[6:8], R)
    time_grad = jnp.sum(step_hot[:, :, None] * time_rows[:, None, :], axis=0)
    upb = own(sums[9 : 9 + FF // 512].reshape(1, FF), F)[0]
    return (
        v["layer_out"], hidden_grad, encoder_grad, time_grad, own(sums[0:3], R), own(sums[3:6], R),
        proj_o, out_o, cq_o, mem_o, co_o, up_o, upb, dn_o, own(sums[8:9], R)[0],
    )


def shards(
    hidden_in, encoder, segment_ids, timestep, out_grad, time_table, norm_gain, norm_bias,
    self_proj, self_out, cross_query, cross_memory, cross_out, up_weight, up_bias, down_weight, down_bias,
):
    S, Z = lax.axis_size("shard"), lax.axis_size("seq")
    s, z = lax.axis_index("shard"), lax.axis_index("seq")
    T, R, F = hidden_in.shape[0], self_proj.shape[0], up_bias.shape[0]
    G = S // 8
    NB = S * Z
    bound = jnp.sum((segment_ids == 0).astype(jnp.int32))
    info = jnp.stack([bound, s // 8, z]).astype(jnp.int32)
    step_hot = timestep[:, None] == jnp.arange(time_table.shape[0], dtype=jnp.int32)[None, :]
    steps = jnp.sum(jnp.where(step_hot[:, :, None], time_table[None], 0), axis=1)
    small = jnp.concatenate(
        [
            jnp.pad(jnp.concatenate([steps, norm_gain, norm_bias], axis=0), ((0, 0), (0, 256 - R))),
            jnp.pad(up_bias[None], ((0, 0), (0, 256 - F))),
            jnp.pad(down_bias[None], ((0, 6), (0, 256 - R))),
        ],
        axis=0,
    ).astype(BF)
    (
        x_all, kv, qt, mkv, enc_all, small_all, vecs, gproj, gmem, gout, gcq, gco, gup, gdn,
    ) = gather_call(
        S, Z, info, hidden_in, small, self_proj, cross_memory, encoder,
        self_out, cross_query, cross_out, up_weight, down_weight,
    )
    wproj, wmem = gproj.reshape(512, 1536), gmem.reshape(512, 1024)
    wout, wcq, wco = gout.reshape(512, 512), gcq.reshape(512, 512), gco.reshape(512, 512)
    wup, wdn = gup.reshape(512, -1), gdn.reshape(-1, 512)
    upb = small_all[:, 8, :F].reshape(1, S * F)
    kv = kv.reshape(NB, T, 128)
    mkv = mkv.reshape(DOCS * ENC // T, T, 128)

    ot, of, lse = attend(Z, True, info, qt, kv)
    at, after, n2, cqt = middle(Z, info, ot, hidden_in, vecs, wout, wcq)
    crt, crf, clse = attend(Z, False, info, cqt, mkv)
    layer_out, d_after2, co_grad, up_grad, dn_grad, small3, upb_grad, dct = feed(
        crt, after, vecs, upb, wco, wup, wdn, out_grad
    )
    dcqt, dmkv = attend_back(Z, False, info, cqt, mkv, dct, crf, clse)
    d_after, cq_grad, wout_grad, small2, dat = middle_back(
        dcqt, after, d_after2, n2, at, vecs, wcq, wout
    )
    dqt, dkv = attend_back(Z, True, info, qt, kv, dat, of, lse)
    return last(locals())


def solution(mesh):
    return jax.shard_map(
        shards,
        mesh=mesh,
        in_specs=(
            P(("shard", "seq"), None),
            P(("shard", "seq"), None),
            P(),
            P(),
            P(("shard", "seq"), None),
            P(None, "shard"),
            P(None, "shard"),
            P(None, "shard"),
            P("shard", None),
            P("shard", None),
            P("shard", None),
            P("shard", None),
            P("shard", None),
            P("shard", None),
            P("shard"),
            P("shard", None),
            P("shard"),
        ),
        out_specs=(
            P(("shard", "seq"), None),
            P(("shard", "seq"), None),
            P(("shard", "seq"), None),
            P(None, "shard"),
            P(None, "shard"),
            P(None, "shard"),
            P("shard", None),
            P("shard", None),
            P("shard", None),
            P("shard", None),
            P("shard", None),
            P("shard", None),
            P("shard"),
            P("shard", None),
            P("shard"),
        ),
        check_vma=False,
    )
```

time: 1120 us -> 505 us (0.45)
  waiting for transfers between devices: 553 us -> 0 us
  Pallas kernels: 0 us -> 473 us
  blocking collectives: 224 us -> 0 us
  matrix products: 99.9 us -> 0 us
  local copies, waits for them, and re-layouts: 111 us -> 19.5 us
  other arithmetic: 52.8 us -> 7.53 us
  starting transfers between devices: 25.5 us -> 0 us
  loops' own time: 24.9 us -> 0 us
  between operations: 19.4 us -> 0.82 us
    pallas_call x0 -> x9, Pallas kernels: none -> 473 us  [the longest x4 291 us: remote_call(): pl.pallas_call(kernel, out_shape=outs, in_specs=in_specs, out_specs=[vmem...]
    reduce_scatter x8 -> x0, waiting for transfers between devices: 359 us -> none  [the longest x1 128 us: shards(): lax.psum_scatter(self_terms.astype(jnp.bfloat16), 'shard', scatter_dimens...]
    all_gather x7 -> x0, blocking collectives: 113 us -> none  [the longest x1 52.4 us: shards(): lax.all_gather(self_out, 'shard', axis=0, tiled=True)]
    dot_general x39 -> x0, matrix products: 99.9 us -> none  [the longest x1 11.2 us: work(): jnp.einsum('hdq,hdk->hqk', grad_heads, value_block, preferred_element_typ...]
    unnamed x25 -> x0, waiting for transfers between devices: 91.2 us -> none
    all_to_all x4 -> x0, blocking collectives: 78.6 us -> none  [the longest x2 39.2 us: to_heads(): lax.all_to_all(stacked, 'seq', split_axis=1, concat_axis=2, tiled=True)]
    psum x1 -> x0, waiting for transfers between devices: 39.7 us -> none  [shards(): lax.psum(memory_part.astype(jnp.bfloat16), 'seq').astype(jnp.float32)]
    all_gather x8 -> x0, waiting for transfers between devices: 37.5 us -> none  [the longest x1 26.1 us: shards(): lax.all_gather(self_heads[2], 'shard', axis=1, tiled=True)]
  transfers between devices with their start and end apart: 27 -> 0, of which waited for: 17 -> 0; matrix products, arithmetic and copies ran while one was open for 22% -> 0% of each run, Pallas kernels for 0% -> 0%
where the time goes in v1:
time: 505 us; the launch traced here: 501 us
  Pallas kernels  473 us (94%)
  local copies, waits for them, and re-layouts  19.5 us (4%)
  other arithmetic  7.53 us (1%)
    pallas_call x4, Pallas kernels, remote_call(): pl.pallas_call(kernel, out_shape=outs, in_specs=in_specs, out_specs=[vmem...  291 us
    pallas_call x1, Pallas kernels, gather_call(): pl.pallas_call(functools.partial(gather_kernel, S, Z, G), out_shape=outs,...  82.4 us
    pallas_call x2, Pallas kernels, attend_back(): pl.pallas_call(functools.partial(attend_back_kernel, Z, causal), out_shap...  52.8 us
    pallas_call x2, Pallas kernels, attend(): pl.pallas_call(functools.partial(attend_kernel, Z, causal), out_shape=[sd...  46.7 us

profile of v1, /device:TPU:0, one launch (start us, length us, event | category | flops | bytes accessed | tf_op | source)
XLA Modules:
  0.0 501.0 jit_solution(7397200210753779297)
XLA Ops:
  0.7 1.4 convert_reduce_fusion
  2.1 1.2 pad_add_fusion.bnd.info
  4.0 0.8 fusion
  6.2 1.3 fusion.2.small
  7.4 82.4 %gather_qkv.1 = (bf16[8,256,512]{2,1,0:T(8,128)(2,1)}, bf16[1,8,4,256,128]{4,3,2,1,0:T(8,128)(2,1)}, bf16[8,64,256]{2,1,0:T(8,128)(2,1)}, bf16[1,8,4,64,128]{4,3...) custom-call(s32[3]{0:T(128)} %pad_add_fusion.bnd.info, ...), custom_call_target="tpu_custom_call" | custom-call | tf_op jit(solution)/shard_map/gather_qkv/pallas_call | solution.py:310
  89.8 30.9 %attend_self.1 = (bf16[8,64,256]{2,1,0:T(8,128)(2,1)}, f32[8,64,256]{2,1,0:T(8,128)}, f32[8,1,256]{2,1,0:T(1,128)}) custom-call(s32[3]{0:T(128)} %pad_add_fusion.bnd.info, bf16[8,64,256]{2,1,0:T(8,128)(2,1)} %get-tuple-element.66.qt, bf16[32,256,128]{2,1,0:T(8,128)(2,1)} %bitcast.23), custom_call_target="tpu_custom_call" | custom-call | tf_op jit(solution)/shard_map/attend_self/pallas_call | solution.py:416
  120.8 15.3 %middle.1 = (bf16[8,64,256]{2,1,0:T(8,128)(2,1)}, f32[256,512]{1,0:T(8,128)}, bf16[256,512]{1,0:T(8,128)(2,1)}, bf16[8,64,256]{2,1,0:T(8,128)(2,1)}) custom-call(s32[3]{0:T(128)} %pad_add_fusion.bnd.info, bf16[8,64,256]{2,1,0:T(8,128)(2,1)} %get-tuple-element.68.ot, bf16[256,512]{1,0:T(8,128)(2,1)} %hid.5, f32[16,512]{1,0:T(8,128)} %get-tuple-element.69.vecs, ...), custom_call_target="tpu_custom_call" | custom-call | tf_op jit(solution)/shard_map/middle/pallas_call | solution.py:573
  136.1 15.8 %attend_cross.1 = (bf16[8,64,256]{2,1,0:T(8,128)(2,1)}, f32[8,64,256]{2,1,0:T(8,128)}, f32[8,1,256]{2,1,0:T(1,128)}) custom-call(s32[3]{0:T(128)} %pad_add_fusion.bnd.info, bf16[8,64,256]{2,1,0:T(8,128)(2,1)} %get-tuple-element.72.qt, bf16[8,256,128]{2,1,0:T(8,128)(2,1)} %bitcast.27), custom_call_target="tpu_custom_call" | custom-call | tf_op jit(solution)/shard_map/attend_cross/pallas_call | solution.py:416
  151.9 1.4 slice.33
  153.2 21.7 %feed_forward.1 = (bf16[256,512]{1,0:T(8,128)(2,1)}, f32[256,512]{1,0:T(8,128)}, bf16[512,512]{1,0:T(8,128)(2,1)}, bf16[512,2048]{1,0:T(8,128)(2,1)}, bf16[2048,...) custom-call(bf16[8,64,256]{2,1,0:T(8,128)(2,1)} %get-tuple-element.74.crt, ...), custom_call_target="tpu_custom_call" | custom-call | tf_op jit(solution)/shard_map/feed_forward/pallas_call | solution.py:573
  174.9 17.8 %attend_cross_back.1 = (bf16[8,64,256]{2,1,0:T(8,128)(2,1)}, bf16[8,256,128]{2,1,0:T(8,128)(2,1)}) custom-call(s32[3]{0:T(128)} %pad_add_fusion.bnd.info, bf16[8,64,256]{2,1,0:T(8,128)(2,1)} %get-tuple-element.72.qt, bf16[8,256,128]{2,1,0:T(8,128)(2,1)} %bitcast.28, bf16[8,64,256]{2,1,0:T(8,128)(2,1)} %get-tuple-element.81.dt, ...), custom_call_target="tpu_custom_call" | custom-call | tf_op jit(solution)/shard_map/attend_cross_back/pallas_call | solution.py:519
  192.7 15.8 %middle_back.1 = (f32[256,512]{1,0:T(8,128)}, bf16[512,512]{1,0:T(8,128)(2,1)}, bf16[512,512]{1,0:T(8,128)(2,1)}, f32[8,512]{1,0:T(8,128)}, bf16[8,64,256]{2,1,0:T(8,128)(2,1)}) custom-call(bf16[8,64,256]{2,1,0:T(8,128)(2,1)} %get-tuple-element.84.dcqt, f32[256,512]{1,0:T(8,128)} %get-tuple-element.75.after, f32[256,512]{1,0:T(8,128)} %get-tuple-element.85.d_after2, ...), custom_call_target="tpu_custom_call" | custom-call | tf_op jit(solution)/shard_map/middle_back/pallas_call | solution.py:573
  208.5 0.8 fusion.11
  210.6 1.3 concatenate.11.smalls_in
  211.8 35.0 %attend_self_back.1 = (bf16[8,64,256]{2,1,0:T(8,128)(2,1)}, bf16[32,256,128]{2,1,0:T(8,128)(2,1)}) custom-call(s32[3]{0:T(128)} %pad_add_fusion.bnd.info, bf16[8,64,256]{2,1,0:T(8,128)(2,1)} %get-tuple-element.66.qt, bf16[32,256,128]{2,1,0:T(8,128)(2,1)} %bitcast.24, bf16[8,64,256]{2,1,0:T(8,128)(2,1)} %get-tuple-element.91.dt, ...), custom_call_target="tpu_custom_call" | custom-call | tf_op jit(solution)/shard_map/attend_self_back/pallas_call | solution.py:519
  246.9 238.5 %gradients_home.1 = (f32[256,512]{1,0:T(8,128)}, f32[64,512]{1,0:T(8,128)}, f32[64,1536]{1,0:T(8,128)}, f32[64,512]{1,0:T(8,128)}, f32[64,512]{1,0:T(8,128)}, /*...) custom-call(s32[3]{0:T(128)} %pad_add_fusion.bnd.info, ...), custom_call_target="tpu_custom_call" | custom-call | tf_op jit(solution)/shard_map/gradients_home/pallas_call | solution.py:573
  485.5 0.8 slice.39
  486.4 0.7 multiply_reduce_fusion
  487.1 0.8 fusion.10
  492.5 1.9 copy.44
  494.4 1.6 copy.45
  496.0 0.7 copy.46
  499.4 0.8 copy.51
  500.2 0.8 copy.52
  (40 shorter events, 10.6 us)
Async XLA Ops:
  174.9 34.9 %copy-start.8 = (f32[1,2048]{1,0:T(1,128)S(1)}, f32[1,2048]{1,0:T(1,128)}, u32[]{:S(2)}) copy-start(f32[1,2048]{1,0:T(1,128)} %get-tuple-element.106) | copy-start | bytes 24580
  246.9 244.9 %copy-start.3 = (bf16[256,512]{1,0:T(8,128)(2,1)S(1)}, bf16[256,512]{1,0:T(8,128)(2,1)}, u32[]{:S(2)}) copy-start(bf16[256,512]{1,0:T(8,128)(2,1)} %get-tuple-element.143) | copy-start | bytes 786436
  485.4 10.6 %copy-start.2 = (f32[64,1536]{1,0:T(8,128)S(1)}, f32[64,1536]{1,0:T(8,128)}, u32[]{:S(2)}) copy-start(f32[64,1536]{1,0:T(8,128)} %get-tuple-element.149) | copy-start | bytes 1179652
  485.4 11.4 %copy-start.7 = (f32[64,512]{1,0:T(8,128)S(1)}, f32[64,512]{1,0:T(8,128)}, u32[]{:S(2)}) copy-start(f32[64,512]{1,0:T(8,128)} %get-tuple-element.150) | copy-start | bytes 393220
  485.4 12.0 %copy-start.6 = (f32[64,512]{1,0:T(8,128)S(1)}, f32[64,512]{1,0:T(8,128)}, u32[]{:S(2)}) copy-start(f32[64,512]{1,0:T(8,128)} %get-tuple-element.151) | copy-start | bytes 393220
  485.4 12.7 %copy-start.4 = (f32[64,1024]{1,0:T(8,128)S(1)}, f32[64,1024]{1,0:T(8,128)}, u32[]{:S(2)}) copy-start(f32[64,1024]{1,0:T(8,128)} %get-tuple-element.152) | copy-start | bytes 786436
  485.4 13.3 %copy-start.5 = (f32[64,512]{1,0:T(8,128)S(1)}, f32[64,512]{1,0:T(8,128)}, u32[]{:S(2)}) copy-start(f32[64,512]{1,0:T(8,128)} %get-tuple-element.153) | copy-start | bytes 393220
  485.4 14.0 %copy-start.1 = (f32[64,2048]{1,0:T(8,128)S(1)}, f32[64,2048]{1,0:T(8,128)}, u32[]{:S(2)}) copy-start(f32[64,2048]{1,0:T(8,128)} %get-tuple-element.154) | copy-start | bytes 1572868
  492.5 7.7 %copy-start = (f32[256,512]{1,0:T(8,128)S(1)}, f32[256,512]{1,0:T(8,128)}, u32[]{:S(2)}) copy-start(f32[256,512]{1,0:T(8,128)} %get-tuple-element.156) | copy-start | bytes 1572868

commit v2 on v1

v2 whole, which is shorter than its diff:
```python
import functools

import jax
import jax.numpy as jnp
from jax import lax
from jax.experimental import pallas as pl
from jax.experimental.pallas import tpu as pltpu
from jax.sharding import PartitionSpec as P

H = 8
HD = 64
DOCS = 2
ENC = 1024
EPS = 1e-05
MASKED = -1e30
SCALE = HD**-0.5
MESH = pl.DeviceIdType.MESH
BF = jnp.bfloat16
F32 = jnp.float32
DMA = pltpu.SemaphoreType.DMA
LIMIT = 62 << 20
ORDER = (0, 1, 2, 4, 3, 6, 5, 7)


def mm(a, b, ca=1, cb=0):
    return lax.dot_general(a, b, (((ca,), (cb,)), ((), ())), preferred_element_type=F32)


def flip(j, bits):
    low, mid, high = j % 2, (j // 2) % 2, (j // 4) % 2
    out = j
    if bits & 1:
        out = out + 1 - 2 * low
    if bits & 2:
        out = out + 2 - 4 * mid
    if bits & 4:
        out = out + 4 - 8 * high
    return out


def rcopy(src, dst, send_sem, recv_sem, device_id):
    return pltpu.make_async_remote_copy(
        src_ref=src,
        dst_ref=dst,
        send_sem=send_sem,
        recv_sem=recv_sem,
        device_id=device_id,
        device_id_type=MESH,
    )


def place():
    shard, seq = lax.axis_index("shard"), lax.axis_index("seq")
    return shard, seq, shard % 8, shard // 8


def greet(peers):
    barrier = pltpu.get_barrier_semaphore()
    count = 0
    for condition, device in peers:
        if condition is None:
            pl.semaphore_signal(barrier, inc=1, device_id=device, device_id_type=MESH)
            count = count + 1
        else:

            @pl.when(condition)
            def _(device=device):
                pl.semaphore_signal(barrier, inc=1, device_id=device, device_id_type=MESH)

            count = count + jnp.where(condition, 1, 0)
    pl.semaphore_wait(barrier, count)


def norm_stats(value):
    center = jnp.mean(value, axis=1, keepdims=True)
    offset = value - center
    spread = jnp.mean(offset * offset, axis=1, keepdims=True)
    scale = lax.rsqrt(spread + EPS)
    return offset * scale, scale


def norm_back(d_out, hat, scale, gain):
    d_hat = d_out * gain
    first = jnp.mean(d_hat, axis=1, keepdims=True)
    second = jnp.mean(d_hat * hat, axis=1, keepdims=True)
    d_in = scale * (d_hat - first - hat * second)
    return d_in, jnp.sum(d_out * hat, axis=0, keepdims=True), jnp.sum(d_out, axis=0, keepdims=True)


def embed(hid_ref, bound, vecs_ref, block):
    rows = hid_ref.shape[0]
    pos = block * rows + lax.broadcasted_iota(jnp.int32, (rows, 1), 0)
    picked = jnp.where(pos < bound, vecs_ref[0:1, :], vecs_ref[1:2, :])
    return hid_ref[...].astype(F32) + picked


class Whole:
    def __init__(self, pairs, S, sems):
        self.pairs, self.S = pairs, S
        self.local, self.send, self.recv, self.half, self.pass_on = sems
        self.s = lax.axis_index("shard")
        self.core, self.chip = self.s % 2, self.s // 2
        self.sib = flip(self.s, 1)
        self.near = S == 8
        self.flow = []

    @staticmethod
    def scratch(count, S):
        return [DMA((count,)), DMA((count, max(8, S // 2))), DMA((count, S)), DMA((count, 2)), DMA((count, S // 2))]

    def copy(self, a, source, n, to, half=None):
        shard, whole = self.pairs[a]
        target = whole.at[source]
        if half is not None:
            rows = shard.shape[0] // 2
            target = whole.at[source, pl.ds(half * rows, rows)]
            recv = self.half.at[a, half]
        else:
            recv = self.recv.at[a, source]
        origin = shard if n < 0 else target
        send = self.send.at[a, -n - 1 if n < 0 else n]
        return rcopy(origin, target, send, recv, {"shard": to})

    def go(self, *args):
        c = self.copy(*args)
        c.start()
        self.flow.append(c)

    def arrived(self, a, source, half=None):
        self.copy(a, source, 7, self.sib, half).wait_recv()

    def same_core(self, d):
        return ((self.chip + d) % (self.S // 2)) * 2 + self.core

    def start(self, a):
        shard, whole = self.pairs[a]
        pltpu.make_async_copy(shard, whole.at[self.s], self.local.at[a]).start()
        s = self.s
        if self.near:
            self.go(a, s, -1, flip(s, 2))
            self.go(a, s, -2, flip(s, 4))
            self.go(a, s, -3, self.sib)
            return
        for d in range(1, self.S // 2):
            c = rcopy(shard, whole.at[s], self.send.at[a, d], self.recv.at[a, s], {"shard": self.same_core(d)})
            c.start()
            self.flow.append(c)
        c = rcopy(shard, whole.at[s], self.send.at[a, 0], self.recv.at[a, s], {"shard": self.sib})
        c.start()
        self.flow.append(c)

    def relay(self, a):
        if not self.near:
            return
        x, y = flip(self.s, 2), flip(self.s, 4)
        self.arrived(a, x)
        self.go(a, x, 3, y, 0)
        self.go(a, x, 5, self.sib)
        self.arrived(a, y)
        self.go(a, y, 4, x, 1)
        self.go(a, y, 6, self.sib)

    def finish(self, a):
        if self.near:
            far = flip(self.s, 6)
            self.arrived(a, far, 0)
            self.arrived(a, far, 1)
            self.go(a, far, 7, self.sib)
            return
        _, whole = self.pairs[a]
        for d in range(1, self.S // 2):
            q = self.same_core(self.S // 2 - d)
            self.arrived(a, q)
            c = rcopy(whole.at[q], whole.at[q], self.pass_on.at[a, d], self.recv.at[a, q], {"shard": self.sib})
            c.start()
            self.flow.append(c)

    def wait(self, a):
        shard, whole = self.pairs[a]
        self.arrived(a, self.sib)
        for d in range(1, self.S // 2):
            self.arrived(a, flip(self.same_core(d), 1))
        pltpu.make_async_copy(shard, whole.at[self.s], self.local.at[a]).wait()

    def drain(self):
        for c in self.flow:
            c.wait_send()


def gather_kernel(
    S, Z, G,
    timestep, seg, hid, table, gain, shift, upb, dnb, wproj, wmem, enc, wout, wcq, wco, wup, wdn,
    info, x_all, kv, qt, mkv, enc_all, vecs, upb_row, gout, gcq, gco, gup, gdn,
    rows_f, small, small_all, wsend, msend, w_all, m_all, sm_s, sm_r, w_s, w_r, mw_s, mw_r,
    x_s, x_r, e_s, e_r, z_s, z_r, mb_s, mb_r, *whole_sems
):
    s, z, j, m = place()
    R, F = wproj.shape[0], upb.shape[1]
    T, E = hid.shape[0], enc.shape[0]
    sib = flip(s, 1)

    step = lax.broadcasted_iota(jnp.int32, table.shape, 0)
    rows_f[...] = jnp.zeros((16, 256), F32)
    for d in range(DOCS):
        picked = jnp.where(step == timestep[d], table[...].astype(F32), 0.0)
        rows_f[d : d + 1, :R] = jnp.sum(picked, axis=0, keepdims=True)
    rows_f[2:5, :R] = gain[...].astype(F32)
    rows_f[5:8, :R] = shift[...].astype(F32)
    rows_f[8:9, :F] = upb[...].astype(F32)
    rows_f[9:10, :R] = dnb[...].astype(F32)
    small[...] = rows_f[...].astype(BF)
    small_all[s] = small[...]
    bound = jnp.sum(jnp.where(seg[...] == 0, 1.0, 0.0)).astype(jnp.int32)
    info[0] = bound
    info[1] = m
    info[2] = z
    info[3] = s

    greet(
        [(None, {"shard": (s + d) % S}) for d in range(1, S)]
        + [(z > 0, {"seq": z - 1}), (z < Z - 1, {"seq": z + 1})]
    )
    small_copies = []
    for d in range(1, S):
        c = rcopy(small, small_all.at[s], sm_s.at[d], sm_r.at[s], {"shard": (s + d) % S})
        c.start()
        small_copies.append(c)
    for h in range(H):
        k = wproj[:, 512 + HD * h : 512 + HD * (h + 1)]
        v = wproj[:, 1024 + HD * h : 1024 + HD * (h + 1)]
        q = wproj[:, HD * h : HD * (h + 1)]
        wsend[h] = jnp.concatenate([k, v, q, jnp.zeros_like(q)], axis=1)
        msend[h] = jnp.concatenate(
            [wmem[:, HD * h : HD * (h + 1)], wmem[:, 512 + HD * h : 512 + HD * (h + 1)]], axis=1
        )
    w_all[s] = wsend[j]
    m_all[s] = msend[j]
    w_copies = []
    for d in range(1, S):
        p = (s + d) % S
        c = rcopy(wsend.at[p % 8], w_all.at[s], w_s.at[d], w_r.at[s], {"shard": p})
        c.start()
        w_copies.append(c)
        c = rcopy(msend.at[p % 8], m_all.at[s], mw_s.at[d], mw_r.at[s], {"shard": p})
        c.start()
        w_copies.append(c)
    for d in range(1, S):
        p = (s + d) % S
        rcopy(small, small_all.at[p], sm_s.at[d], sm_r.at[p], {"shard": p}).wait_recv()
    rows = jnp.zeros((16, 512), F32)
    lane = lax.broadcasted_iota(jnp.int32, (256, 512), 0)
    col = lax.broadcasted_iota(jnp.int32, (256, 512), 1)
    for p in range(S):
        pick = ((col - p * R) == lane) & (lane < R)
        rows = rows + mm(small_all[p], jnp.where(pick, 1.0, 0.0).astype(BF))
        upb_row[0:1, p * F : (p + 1) * F] = small_all[p].astype(F32)[8:9, :F]
    vecs[...] = rows

    hat, _ = norm_stats(embed(hid, bound, vecs, s * Z + z))
    x_all[j] = (hat * vecs[2:3, :] + vecs[5:6, :]).astype(BF)
    enc_all[j] = enc[...]
    copies = []

    def send_block(ref, bits_source, bits_target, send, recv):
        source = flip(j, bits_source)
        c = rcopy(ref.at[source], ref.at[source], send, recv.at[source], {"shard": flip(s, bits_target)})
        c.start()
        copies.append(c)

    def wait_block(ref, bits, recv):
        source = flip(j, bits)
        rcopy(ref.at[source], ref.at[source], x_s.at[0], recv.at[source], {"shard": sib}).wait_recv()

    for n, bits in enumerate((1, 2, 4, 6)):
        send_block(x_all, 0, bits, x_s.at[n], x_r)
    for n, bits in enumerate((1, 2, 4, 6)):
        send_block(enc_all, 0, bits, e_s.at[n], e_r)
    whole = Whole(
        ((wout, gout), (wcq, gcq), (wco, gco), (wup, gup), (wdn, gdn)), S, whole_sems
    )
    for a in range(3):
        whole.start(a)
    for d in range(1, S):
        p = (s + d) % S
        rcopy(wsend.at[0], w_all.at[p], w_s.at[d], w_r.at[p], {"shard": p}).wait_recv()
        rcopy(msend.at[0], m_all.at[p], mw_s.at[d], mw_r.at[p], {"shard": p}).wait_recv()
    w_head = w_all[...].reshape(S * R, 256)
    m_head = m_all[...].reshape(S * R, 128)

    def z_copy(ref, block, plane, step, hop, slot):
        view = ref.at[:, block, plane] if block is not None else ref.at[:, :, plane]
        way = (step + 1) // 2
        return rcopy(view, view, z_s.at[way, hop, slot], z_r.at[way, hop, slot], {"seq": z + step})

    def z_passes(step, hop):
        origin = z - step * hop
        return (z + step >= 0) & (z + step < Z) & (origin >= 0) & (origin < Z)

    def z_send(ref, block, hop, slot):
        for step in (-1, 1):

            @pl.when(z_passes(step, hop))
            def _(step=step):
                z_copy(ref, block, z - step * hop, step, hop, slot).start()

    def z_recv(ref, block, hop, slot):
        for step in (-1, 1):
            origin = z - step * hop

            @pl.when((origin >= 0) & (origin < Z))
            def _(step=step, origin=origin):
                z_copy(ref, block, origin, step, hop - 1, slot).wait_recv()

    def z_drain(ref, block, hop, slot):
        for step in (-1, 1):

            @pl.when(z_passes(step, hop))
            def _(step=step):
                z_copy(ref, block, z - step * hop, step, hop, slot).wait_send()

    def member_copy(ref, block, d, slot, mine):
        other = (m + d) % G
        at = m if mine else other
        view = ref.at[at, block, z] if block is not None else ref.at[at, :, z]
        return rcopy(view, view, mb_s.at[d, slot], mb_r.at[at, slot], {"shard": other * 8 + j})

    def spread(ref, block, slot):
        for d in range(1, G):
            member_copy(ref, block, d, slot, True).start()
        for d in range(1, G):
            member_copy(ref, block, d, slot, False).wait_recv()
        z_send(ref, block, 0, slot)

    for n, bits in enumerate(ORDER):
        block = flip(j, bits)
        if bits:
            wait_block(x_all, bits, x_r)
            if bits in (2, 4, 6):
                send_block(x_all, bits, 1, x_s.at[3 + bits // 2], x_r)
        kvq = mm(x_all[block], w_head)
        kv[m, block, z] = kvq[:, :128].astype(BF)
        spread(kv, block, n)
        qt[block] = (SCALE * kvq[:, 128:256].T[:HD]).astype(BF)
    for a in range(3, 5):
        whole.start(a)

    for bits in (2, 4, 6):
        wait_block(enc_all, bits, e_r)
        send_block(enc_all, bits, 1, e_s.at[3 + bits // 2], e_r)
    for bits in (1, 3, 5, 7):
        wait_block(enc_all, bits, e_r)
    for b in range(8):
        mkv[m, b, z] = mm(enc_all[b], m_head).astype(BF)
    spread(mkv, None, 8)

    for hop in range(1, Z):
        for n, bits in enumerate(ORDER):
            z_recv(kv, flip(j, bits), hop, n)
            z_send(kv, flip(j, bits), hop, n)
        z_recv(mkv, None, hop, 8)
        z_send(mkv, None, hop, 8)
        if hop == 1:
            for a in range(3):
                whole.relay(a)
        if hop == min(2, Z - 1):
            for a in range(3, 5):
                whole.relay(a)
            for a in range(3):
                whole.finish(a)
    for a in range(3, 5):
        whole.finish(a)
    for a in range(5):
        whole.wait(a)
    whole.drain()
    for c in small_copies + w_copies + copies:
        c.wait_send()
    for n, bits in enumerate(ORDER):
        for d in range(1, G):
            member_copy(kv, flip(j, bits), d, n, True).wait_send()
        for hop in range(Z - 1):
            z_drain(kv, flip(j, bits), hop, n)
    for d in range(1, G):
        member_copy(mkv, None, d, 8, True).wait_send()
    for hop in range(Z - 1):
        z_drain(mkv, None, hop, 8)


def gather_call(S, Z, args):
    G = S // 8
    (timestep, seg, hid, table, gain, shift, upb, dnb, wproj, wmem, enc, *weights) = args
    T, R, E, F = hid.shape[0], wproj.shape[0], enc.shape[0], upb.shape[1]
    vmem = pl.BlockSpec(memory_space=pltpu.VMEM)
    smem = pl.BlockSpec(memory_space=pltpu.SMEM)
    hbm = pl.BlockSpec(memory_space=pl.ANY)
    sds = jax.ShapeDtypeStruct
    outs = [
        sds((4,), jnp.int32),
        sds((8, T, 512), BF),
        sds((G, 8, Z, T, 128), BF),
        sds((8, HD, T), BF),
        sds((G, 8, Z, E, 128), BF),
        sds((8, E, 512), BF),
        sds((16, 512), F32),
        sds((1, S * F), F32),
    ] + [sds((S,) + w.shape, BF) for w in weights]
    return pl.pallas_call(
        functools.partial(gather_kernel, S, Z, G),
        out_shape=outs,
        in_specs=[smem] + [vmem] * (len(args) - 1),
        out_specs=[smem] + [vmem] * 7 + [hbm] * 5,
        scratch_shapes=[
            pltpu.VMEM((16, 256), F32),
            pltpu.VMEM((16, 256), BF),
            pltpu.VMEM((S, 16, 256), BF),
            pltpu.VMEM((8, R, 256), BF),
            pltpu.VMEM((8, R, 128), BF),
            pltpu.VMEM((S, R, 256), BF),
            pltpu.VMEM((S, R, 128), BF),
            DMA((S,)), DMA((S,)), DMA((S,)), DMA((S,)), DMA((S,)), DMA((S,)),
            DMA((8,)), DMA((8,)), DMA((8,)), DMA((8,)),
            DMA((2, Z, 9)), DMA((2, Z, 9)),
            DMA((G, 9)), DMA((G, 9)),
        ] + Whole.scratch(5, S),
        compiler_params=pltpu.CompilerParams(
            collective_id=0, has_side_effects=True, vmem_limit_bytes=LIMIT
        ),
        name="gather_qkv",
    )(*args)


GROUP = 4


class Reach:
    def __init__(self, causal, bound, block, rows):
        self.causal, self.bound, self.rows = causal, bound, rows
        self.query_first = block * rows
        last = self.query_first + rows - 1
        mixed = (self.query_first < bound) & (last >= bound)
        if causal:
            self.least = jnp.where(self.query_first < bound, 0, bound)
            begin, self.end = self.least // rows, block + 1
            self.mixed = mixed | (self.end < GROUP)
        else:
            per = ENC // rows
            self.least = 0
            begin = jnp.where(self.query_first < bound, 0, per)
            self.end = jnp.where(last < bound, per, 2 * per)
            self.mixed = mixed
        self.groups = (self.end - begin + GROUP - 1) // GROUP

    def mask(self, kind, start, limit, n, scores):
        if kind == "plain":
            return scores
        rows = self.rows
        key = (start + n) * rows + lax.broadcasted_iota(jnp.int32, (rows, 1), 0)
        query = self.query_first + lax.broadcasted_iota(jnp.int32, (1, scores.shape[1]), 1)
        if kind == "edge":
            allowed = (key >= self.least) & (key < limit)
            if n == GROUP - 1:
                allowed = allowed & (key <= query)
        elif self.causal:
            least = jnp.where(query < self.bound, 0, self.bound)
            allowed = (key < limit) & (key <= query) & (key >= least)
        else:
            allowed = jnp.where(query < self.bound, 0, 1) == key // ENC
        return jnp.where(allowed, scores, MASKED)

    def walk(self, group, state):
        def turn(kind, g, carry):
            if kind == "edge":
                g = jnp.where(g == 0, 0, self.groups - 1)
            stop = self.end - GROUP * (self.groups - 1 - g)
            return group(kind, jnp.maximum(stop - GROUP, 0), stop * self.rows, carry)

        mixed, groups = self.mixed, self.groups
        state = lax.fori_loop(
            0, jnp.where(mixed, groups, 0), functools.partial(turn, "full"), state
        )
        if not self.causal:
            return lax.fori_loop(
                0, jnp.where(mixed, 0, groups), functools.partial(turn, "plain"), state
            )
        state = lax.fori_loop(
            0,
            jnp.where(mixed, 0, jnp.minimum(groups, 2)),
            functools.partial(turn, "edge"),
            state,
        )
        return lax.fori_loop(
            1, jnp.where(mixed, 1, groups - 1), functools.partial(turn, "plain"), state
        )


def turned_keys(kv, kt, half, begin, end):
    rows = kv.shape[1]

    def turn(kb, carry):
        flat = kv[kb].astype(F32).T[HD * half : HD * (half + 1)].astype(BF)
        kt[:, pl.ds(pl.multiple_of(kb * rows, rows), rows)] = flat
        return carry

    lax.fori_loop(begin, end, turn, 0)


def key_span(causal, bound, low, Z, rows, count):
    if not causal:
        return 0, count
    return jnp.where(low * rows < bound, 0, bound) // rows, low + 7 * Z + 1


def attend_kernel(Z, causal, info, qt, kv, ot, of, lse, vt):
    bound, m, z = info[0], info[1], info[2]
    count, T = kv.shape[0], kv.shape[1]
    low = 8 * m * Z + z

    begin, end = key_span(causal, bound, low, Z, T, count)
    turned_keys(kv, vt, 1, jnp.maximum(begin - GROUP, 0), end)

    def one_block(i, carry):
        reach = Reach(causal, bound, low + i * Z, T)
        queries = jnp.concatenate([qt[i], jnp.zeros((HD, T), BF)], axis=0)

        def group(kind, start, limit, state):
            top, total, acc = state
            keys = kv[pl.ds(start, GROUP)].reshape(GROUP * T, 128)
            raw = mm(keys, queries)
            scores = [
                reach.mask(kind, start, limit, n, raw[n * T : (n + 1) * T]) for n in range(GROUP)
            ]
            new_top = top
            for piece in scores:
                new_top = jnp.maximum(new_top, jnp.max(piece, axis=0, keepdims=True))
            fade = jnp.exp(top - new_top)
            total = total * fade
            parts = []
            for piece in scores:
                powers = jnp.exp(piece - new_top)
                total = total + jnp.sum(powers, axis=0, keepdims=True)
                parts.append(powers.astype(BF))
            values = vt[:, pl.ds(pl.multiple_of(start * T, T), GROUP * T)]
            acc = acc * fade + mm(values, jnp.concatenate(parts, axis=0))
            return new_top, total, acc

        top, total, acc = reach.walk(
            group,
            (jnp.full((1, T), MASKED, F32), jnp.zeros((1, T), F32), jnp.zeros((HD, T), F32)),
        )
        result = acc / total
        ot[i] = result.astype(BF)
        of[i] = result
        lse[i] = top + jnp.log(total)
        return carry

    lax.fori_loop(0, 8, one_block, 0)


def attend(Z, causal, info, qt, kv):
    T = qt.shape[2]
    sds = jax.ShapeDtypeStruct
    vmem = pl.BlockSpec(memory_space=pltpu.VMEM)
    return pl.pallas_call(
        functools.partial(attend_kernel, Z, causal),
        out_shape=[sds((8, HD, T), BF), sds((8, HD, T), F32), sds((8, 1, T), F32)],
        in_specs=[pl.BlockSpec(memory_space=pltpu.SMEM), vmem, vmem],
        out_specs=[vmem] * 3,
        scratch_shapes=[pltpu.VMEM((HD, kv.shape[0] * T), BF)],
        compiler_params=pltpu.CompilerParams(vmem_limit_bytes=LIMIT),
        name="attend_self" if causal else "attend_cross",
    )(info, qt, kv)


def attend_back_kernel(
    Z, causal, info, qt, kv, dt, of, lse, dq, dkv, kt, dkvf, qd, rows, raw, pair, stage, sem
):
    bound, m, z = info[0], info[1], info[2]
    count, T = kv.shape[0], kv.shape[1]
    low = 8 * m * Z + z
    zero = jnp.zeros((HD, T), BF)

    def clear(kb, carry):
        dkvf[kb] = jnp.zeros((T, 128), F32)
        return carry

    lax.fori_loop(0, count, clear, 0)

    begin, end = key_span(causal, bound, low, Z, T, count)
    turned_keys(kv, kt, 0, jnp.maximum(begin - GROUP, 0), end)

    def one_block(i, carry):
        reach = Reach(causal, bound, low + i * Z, T)
        qd[:HD, :T] = qt[i]
        qd[HD:, :T] = zero
        qd[:HD, T:] = zero
        qd[HD:, T:] = dt[i]
        both = jnp.concatenate([qt[i].astype(F32), dt[i].astype(F32)], axis=0).T
        lane = lax.broadcasted_iota(jnp.int32, both.shape, 1)
        rows[:T] = jnp.where(lane < HD, 0.0, both).astype(BF)
        rows[T:] = jnp.where(lane < HD, both, 0.0).astype(BF)
        delta = jnp.sum(dt[i].astype(F32) * of[i], axis=0, keepdims=True)
        level = lse[i]

        def group(kind, start, limit, acc):
            keys = kv[pl.ds(start, GROUP)].reshape(GROUP * T, 128)
            raw[...] = mm(keys, qd[...])
            for n in range(GROUP):
                at = slice(n * T, (n + 1) * T)
                probs = jnp.exp(reach.mask(kind, start, limit, n, raw[at, :T]) - level)
                pair[at, :T] = probs.astype(BF)
                pair[at, T:] = (probs * (raw[at, T:] - delta)).astype(BF)
            grads = mm(pair[...], rows[...])
            dkvf[pl.ds(start, GROUP)] += grads.reshape(GROUP, T, 128)
            flat = kt[:, pl.ds(pl.multiple_of(start * T, T), GROUP * T)]
            return acc + mm(flat, pair[:, T:])

        acc = reach.walk(group, jnp.zeros((HD, T), F32))
        dq[i] = (SCALE * acc).astype(BF)
        return carry

    lax.fori_loop(0, 8, one_block, 0)

    def put(kb):
        return pltpu.make_async_copy(stage.at[kb % 2], dkv.at[kb], sem.at[kb % 2])

    def flush(kb, carry):
        @pl.when(kb >= 2)
        def _():
            put(kb).wait()

        stage[kb % 2] = dkvf[kb].astype(BF)
        put(kb).start()
        return carry

    lax.fori_loop(0, count, flush, 0)
    put(0).wait()
    put(1).wait()


def attend_back(Z, causal, info, qt, kv, dt, of, lse):
    T = qt.shape[2]
    count = kv.shape[0]
    sds = jax.ShapeDtypeStruct
    vmem = pl.BlockSpec(memory_space=pltpu.VMEM)
    return pl.pallas_call(
        functools.partial(attend_back_kernel, Z, causal),
        out_shape=[sds((8, HD, T), BF), sds(kv.shape, BF)],
        in_specs=[pl.BlockSpec(memory_space=pltpu.SMEM)] + [vmem] * 5,
        out_specs=[vmem, pl.BlockSpec(memory_space=pl.ANY)],
        scratch_shapes=[
            pltpu.VMEM((HD, count * T), BF),
            pltpu.VMEM((count, T, 128), F32),
            pltpu.VMEM((128, 2 * T), BF),
            pltpu.VMEM((2 * T, 128), BF),
            pltpu.VMEM((GROUP * T, 2 * T), F32),
            pltpu.VMEM((GROUP * T, 2 * T), BF),
            pltpu.VMEM((2, T, 128), BF),
            DMA((2,)),
        ],
        compiler_params=pltpu.CompilerParams(vmem_limit_bytes=LIMIT),
        name="attend_self_back" if causal else "attend_cross_back",
    )(info, qt, kv, dt, of, lse)


def greet_group():
    s, z, j, m = place()
    greet([(None, {"shard": m * 8 + (j + d) % 8}) for d in range(1, 8)])


def exchange_copies(src, dst, send, recv):
    s, z, j, m = place()
    out = []
    for d in (1, 2, 3, 4, 5, 6, 7):
        p = flip(j, d)
        out.append(rcopy(src.at[p], dst.at[j], send.at[d], recv.at[j], {"shard": m * 8 + p}))
    return out


def exchange_start(src, dst, send, recv):
    s, z, j, m = place()
    for c in exchange_copies(src, dst, send, recv):
        c.start()
    dst[j] = src[j]


def exchange_recv(src, dst, send, recv):
    s, z, j, m = place()
    for d in (1, 2, 3, 4, 5, 6, 7):
        p = flip(j, d)
        rcopy(src.at[p], dst.at[p], send.at[d], recv.at[p], {"shard": m * 8 + p}).wait_recv()


def exchange_sent(src, dst, send, recv):
    for c in exchange_copies(src, dst, send, recv):
        c.wait_send()


def remote_call(kernel, name, ident, ins, outs, scratch, smem=1, far=()):
    vmem = pl.BlockSpec(memory_space=pltpu.VMEM)
    in_specs = [pl.BlockSpec(memory_space=pltpu.SMEM)] * smem + [vmem] * (len(ins) - smem)
    for n in far:
        in_specs[n] = pl.BlockSpec(memory_space=pl.ANY)
    return pl.pallas_call(
        kernel,
        out_shape=outs,
        in_specs=in_specs,
        out_specs=[vmem] * len(outs),
        scratch_shapes=scratch,
        compiler_params=pltpu.CompilerParams(
            collective_id=ident, has_side_effects=True, vmem_limit_bytes=LIMIT
        ),
        name=name,
    )(*ins)


def middle_kernel(Z, bnd, ot, hid, vecs, wout, wcq, at, after, n2, cqt, cq_send, s1, r1, s2, r2):
    s, z, j, m = place()
    T = hid.shape[0]
    greet_group()
    exchange_start(ot, at, s1, r1)
    base = embed(hid, bnd[0], vecs, s * Z + z)
    exchange_recv(ot, at, s1, r1)
    attn = at[...].reshape(512, T).astype(F32).T.astype(BF)
    value = base + mm(attn, wout[...])
    after[...] = value
    hat, _ = norm_stats(value)
    normed = (hat * vecs[3:4, :] + vecs[6:7, :]).astype(BF)
    n2[...] = normed
    cq = mm(normed, wcq[...])
    cq_send[...] = (SCALE * cq.T).astype(BF).reshape(8, HD, T)
    exchange_start(cq_send, cqt, s2, r2)
    exchange_recv(cq_send, cqt, s2, r2)
    exchange_sent(ot, at, s1, r1)
    exchange_sent(cq_send, cqt, s2, r2)


def middle(Z, bnd, ot, hid, vecs, wout, wcq):
    T = hid.shape[0]
    sds = jax.ShapeDtypeStruct
    return remote_call(
        functools.partial(middle_kernel, Z),
        "middle",
        1,
        (bnd, ot, hid, vecs, wout, wcq),
        [sds((8, HD, T), BF), sds((T, 512), F32), sds((T, 512), BF), sds((8, HD, T), BF)],
        [pltpu.VMEM((8, HD, T), BF), DMA((8,)), DMA((8,)), DMA((8,)), DMA((8,))],
    )


def erf(x):
    return lax.erf(x)


def feed_kernel(
    crt, after, vecs, upb, wco, wup, wdn, grad,
    layer_out, d_after, co_grad, up_grad, dn_grad, smalls, upb_grad, dct,
    ct, send, n3t, out_acc, dn_acc, s1, r1, s2, r2,
):
    T = after.shape[0]
    FF = wup.shape[1]
    greet_group()
    exchange_start(crt, ct, s1, r1)
    g = grad[...]
    gf = g.astype(F32)
    gt = gf.T.astype(BF)
    exchange_recv(crt, ct, s1, r1)
    cross_t = ct[...].reshape(512, T)
    value = after[...] + mm(cross_t.astype(F32).T.astype(BF), wco[...])
    hat, scale = norm_stats(value)
    normed = hat * vecs[4:5, :] + vecs[7:8, :]
    n3 = normed.astype(BF)
    n3t[...] = n3.astype(F32).T.astype(BF)
    out_acc[...] = value + vecs[9:10, :]
    dn_acc[...] = jnp.zeros_like(dn_acc)
    width = 512
    for c in range(FF // width):
        lo, hi = c * width, (c + 1) * width
        pre = mm(n3, wup[:, lo:hi]) + upb[0:1, lo:hi]
        half = 0.5 * (1.0 + erf(pre * (0.5**0.5)))
        middle_c = (pre * half).astype(BF)
        out_acc[...] += mm(middle_c, wdn[lo:hi, :])
        slope = half + pre * (jnp.exp(-0.5 * pre * pre) * ((0.5 / jnp.pi) ** 0.5))
        d_pre = mm(g, wdn[lo:hi, :], 1, 1) * slope
        d_pre_b = d_pre.astype(BF)
        upb_grad[0:1, lo:hi] = jnp.sum(d_pre_b.astype(F32), axis=0, keepdims=True)
        dn_grad[lo:hi, :] = mm(middle_c.astype(F32).T.astype(BF), g).astype(BF)
        up_grad[:, lo:hi] = mm(n3t[...], d_pre_b).astype(BF)
        dn_acc[...] += mm(d_pre_b, wup[:, lo:hi], 1, 1)
    layer_out[...] = out_acc[...].astype(BF)
    d_value, d_gain, d_shift = norm_back(dn_acc[...], hat, scale, vecs[4:5, :])
    total = gf + d_value
    d_after[...] = total
    smalls[0:1, :] = d_gain
    smalls[1:2, :] = d_shift
    smalls[2:3, :] = jnp.sum(gf, axis=0, keepdims=True)
    dc = total.astype(BF)
    d_cross = mm(wco[...], dc, 1, 1)
    send[...] = d_cross.astype(BF).reshape(8, HD, T)
    exchange_start(send, dct, s2, r2)
    co_grad[...] = mm(cross_t, dc).astype(BF)
    exchange_recv(send, dct, s2, r2)
    exchange_sent(crt, ct, s1, r1)
    exchange_sent(send, dct, s2, r2)


def feed(crt, after, vecs, upb, wco, wup, wdn, grad):
    T, FF = after.shape[0], wup.shape[1]
    sds = jax.ShapeDtypeStruct
    return remote_call(
        feed_kernel,
        "feed_forward",
        2,
        (crt, after, vecs, upb, wco, wup, wdn, grad),
        [
            sds((T, 512), BF),
            sds((T, 512), F32),
            sds((512, 512), BF),
            sds((512, FF), BF),
            sds((FF, 512), BF),
            sds((8, 512), F32),
            sds((1, FF), F32),
            sds((8, HD, T), BF),
        ],
        [
            pltpu.VMEM((8, HD, T), BF),
            pltpu.VMEM((8, HD, T), BF),
            pltpu.VMEM((512, T), BF),
            pltpu.VMEM((T, 512), F32),
            pltpu.VMEM((T, 512), F32),
            DMA((8,)), DMA((8,)), DMA((8,)), DMA((8,)),
        ],
        smem=0,
    )


def middle_back_kernel(
    dcqt, after, d_after2, n2, at, vecs, wcq, wout,
    d_after, cq_grad, out_grad, smalls, dat,
    home, send, s1, r1, s2, r2,
):
    T = after.shape[0]
    greet_group()
    exchange_start(dcqt, home, s1, r1)
    hat, scale = norm_stats(after[...])
    n2t = n2[...].astype(F32).T.astype(BF)
    exchange_recv(dcqt, home, s1, r1)
    dcq = home[...].reshape(512, T).astype(F32).T.astype(BF)
    d_value, d_gain, d_shift = norm_back(mm(dcq, wcq[...], 1, 1), hat, scale, vecs[3:4, :])
    total = d_after2[...] + d_value
    d_after[...] = total
    smalls[0:1, :] = d_gain
    smalls[1:2, :] = d_shift
    da = total.astype(BF)
    send[...] = mm(wout[...], da, 1, 1).astype(BF).reshape(8, HD, T)
    exchange_start(send, dat, s2, r2)
    cq_grad[...] = mm(n2t, dcq).astype(BF)
    out_grad[...] = mm(at[...].reshape(512, T), da).astype(BF)
    exchange_recv(send, dat, s2, r2)
    exchange_sent(dcqt, home, s1, r1)
    exchange_sent(send, dat, s2, r2)


def middle_back(dcqt, after, d_after2, n2, at, vecs, wcq, wout):
    T = after.shape[0]
    sds = jax.ShapeDtypeStruct
    return remote_call(
        middle_back_kernel,
        "middle_back",
        3,
        (dcqt, after, d_after2, n2, at, vecs, wcq, wout),
        [
            sds((T, 512), F32),
            sds((512, 512), BF),
            sds((512, 512), BF),
            sds((8, 512), F32),
            sds((8, HD, T), BF),
        ],
        [
            pltpu.VMEM((8, HD, T), BF),
            pltpu.VMEM((8, HD, T), BF),
            DMA((8,)), DMA((8,)), DMA((8,)), DMA((8,)),
        ],
        smem=0,
    )


NC = 16


def last_kernel(
    S, Z, G,
    info, hid, vecs, d_after, x_all, enc_all, dqt, dkv, dmkv, wproj_s, wmem_s,
    out_g, cq_g, co_g, up_g, dn_g, small2, small3, upb_g,
    hidden_grad, encoder_grad, zfin, smalls_o,
    wproj_all, wmem_all,
    sib_out, sib_cq, sib_co, sib_up, sib_dn, got_out, got_cq, got_co, got_up, got_dn,
    rk, rm, fin, finm, mbuf, mbufm, hkv, hq, hm, turned, enc_turned, dall, psend, pgot, msend, mgot,
    wz, zin, sm_all, sm_z, sm_plane, sm_mine,
    a_s, a_r, b_s, b_r, k_s, k_r, mb_s, mb_r, hq_s, hq_r, hk_s, hk_r, hm_s, hm_r,
    p_s, p_r, pm_s, pm_r, c_s, c_r, f_s, f_r, sm_s, sm_r, sz_s, sz_r, *whole_sems
):
    s, z, j, m = place()
    T, E = hid.shape[0], enc_all.shape[1]
    R = 512 // S
    F = dn_g.shape[0] // S
    bound = info[0]
    chips = S // 2
    core, chip = s % 2, s // 2
    sib = flip(s, 1)
    ends = (Z - 1, 0)
    greet(
        [(None, {"shard": (s + d) % S}) for d in range(1, S)]
        + [(None, {"seq": (z + d) % Z}) for d in range(1, Z)]
    )
    grads = ((out_g, R), (cq_g, R), (co_g, R), (up_g, R), (dn_g, F))
    sibs = (sib_out, sib_cq, sib_co, sib_up, sib_dn)
    gots = (got_out, got_cq, got_co, got_up, got_dn)

    def piece(a, p):
        ref, rows = grads[a]
        return ref.at[pl.ds(pl.multiple_of(p * rows, rows), rows), :]

    if G > 1:
        for d in range(1, G):
            o = (m + d) % G
            rcopy(dkv.at[o], mbuf.at[m], mb_s.at[d, 0], mb_r.at[m, 0], {"shard": o * 8 + j}).start()
            rcopy(dmkv.at[o], mbufm.at[m], mb_s.at[d, 1], mb_r.at[m, 1], {"shard": o * 8 + j}).start()
        own_part = pltpu.make_async_copy(dkv.at[m], mbuf.at[m], mb_s.at[0, 0])
        own_part.start()
        own_part.wait()
        for d in range(1, G):
            o = (m + d) % G
            rcopy(dkv.at[o], mbuf.at[o], mb_s.at[d, 0], mb_r.at[o, 0], {"shard": o * 8 + j}).wait_recv()
            rcopy(dmkv.at[o], mbufm.at[o], mb_s.at[d, 1], mb_r.at[o, 1], {"shard": o * 8 + j}).wait_recv()
        for b in range(8):
            acc = mbuf[m, b].astype(F32)
            accm = dmkv[m, b].astype(F32)
            for d in range(1, G):
                acc = acc + mbuf[(m + d) % G, b].astype(F32)
                accm = accm + mbufm[(m + d) % G, b].astype(F32)
            mbuf[m, b] = acc.astype(BF)
            mbufm[m, b] = accm.astype(BF)
        part, partm = mbuf.at[m], mbufm.at[m]
    else:
        part, partm = dkv.at[0], dmkv.at[0]

    def z_view(slot, t):
        return part.at[slot, t] if slot < 8 else partm.at[:, t]

    def z_buffer(way, t, slot):
        return rk.at[way, t, slot] if slot < 8 else rm.at[way, t]

    def z_copy(way, t, slot, source):
        step = 2 * way - 1
        return rcopy(
            source, z_buffer(way, t, slot), k_s.at[way, t, slot], k_r.at[way, t, slot], {"seq": z + step}
        )

    for far in range(Z - 1, 0, -1):
        for slot in range(9):
            for way in (0, 1):
                t = z + (2 * way - 1) * far

                @pl.when((z == ends[way]) & (t >= 0) & (t < Z))
                def _(way=way, t=t, slot=slot):
                    z_copy(way, t, slot, z_view(slot, t)).start()

    def sib_copy(a, q):
        return rcopy(piece(a, 2 * q + 1 - core), sibs[a].at[q], a_s.at[a, q], a_r.at[a, q], {"shard": sib})

    for a in range(5):
        for q in range(chips):
            sib_copy(a, q).start()
    exchange_start(dqt, hq, hq_s, hq_r)
    whole = Whole(((wproj_s, wproj_all), (wmem_s, wmem_all)), S, whole_sems)

    def own_copy(a, q):
        return rcopy(
            sibs[a].at[q], gots[a].at[chip], b_s.at[a, q], b_r.at[a, chip], {"shard": 2 * q + core}
        )

    def chip_sum(a):
        for d in range(chips):
            q = (chip + d + 1) % chips
            sib_copy(a, q).wait_recv()
            sibs[a][q] = (
                sibs[a][q].astype(F32) + piece(a, 2 * q + core)[...].astype(F32)
            ).astype(BF)
            if d < chips - 1:
                own_copy(a, q).start()

    def turn_block(b):
        turned[:, b * T : (b + 1) * T] = x_all[b].astype(F32).T.astype(BF)

    def turn_query(b):
        dq_b = dqt[b].astype(F32)
        dall[b * T : (b + 1) * T, 128:] = (
            jnp.concatenate([dq_b, jnp.zeros_like(dq_b)], axis=0).T.astype(BF)
        )

    def turn_encoder():
        enc_turned[...] = enc_all[...].reshape(8 * E, 512).astype(F32).T.astype(BF)

    def start_whole():
        whole.start(0)
        whole.start(1)

    def relay_whole():
        whole.relay(0)
        whole.relay(1)

    def finish_whole():
        whole.finish(0)
        whole.finish(1)

    def own_sum(a):
        for d in range(1, chips):
            q = (chip + d) % chips
            rcopy(sibs[a].at[q], gots[a].at[q], b_s.at[a, q], b_r.at[a, q], {"shard": 2 * q + core}).wait_recv()
        total = sibs[a][chip].astype(F32)
        for d in range(1, chips):
            total = total + gots[a][(chip + d) % chips].astype(F32)
        total = total.astype(BF)
        if a < 3:
            wz[a] = total
        elif a == 3:
            for c in range(4):
                wz[3 + c] = total[:, 512 * c : 512 * (c + 1)]
        else:
            for c in range(4):
                wz[7 + c] = total[c * R : (c + 1) * R]

    block = s * Z + z
    work = [functools.partial(chip_sum, a) for a in range(5)] + [start_whole]
    work += [functools.partial(turn_block, b) for b in range(8)]
    work += [functools.partial(turn_query, b) for b in range(8)] + [turn_encoder]
    late = [relay_whole, finish_whole]

    for far in range(Z - 1, 0, -1):
        for slot in range(9):
            if work:
                work.pop(0)()
            for way in (0, 1):
                t = z + (2 * way - 1) * far

                @pl.when((z != ends[way]) & (t >= 0) & (t < Z))
                def _(way=way, t=t, slot=slot):
                    z_copy(way, t, slot, z_view(slot, t)).wait_recv()
                    buf = z_buffer(way, t, slot)
                    buf[...] = (
                        buf[...].astype(F32) + z_view(slot, t)[...].astype(F32)
                    ).astype(BF)
                    z_copy(way, t, slot, buf).start()

    def inward(k, step):
        way = (step + 1) // 2
        return rcopy(wz.at[k], zin.at[way, k], c_s.at[way, k], c_r.at[way, k], {"seq": z + step})

    def outward(k, step):
        return rcopy(zfin.at[k], zfin.at[k], f_s.at[(step + 1) // 2, k], f_r.at[k], {"seq": z + step})

    def root(k):
        return max(Z // 2 - 1 + k % 2, 0) if Z > 1 else 0

    def tips(k):
        r = root(k)
        for step in (-1, 1):
            tip = ends[(step + 1) // 2]
            if tip != r:

                @pl.when(z == tip)
                def _(step=step):
                    inward(k, step).start()

    def partial(k):
        r = root(k)
        for step, beyond in ((-1, z > r), (1, z < r)):
            tip = ends[(step + 1) // 2]
            way = (step + 1) // 2

            @pl.when(beyond & (z != tip))
            def _(step=step, way=way):
                inward(k, step).wait_recv()
                wz[k] = (wz[k].astype(F32) + zin[way, k].astype(F32)).astype(BF)
                inward(k, step).start()

    def total_of(k):
        r = root(k)

        @pl.when(z == r)
        def _():
            total = wz[k].astype(F32)
            if r < Z - 1:
                inward(k, -1).wait_recv()
                total = total + zin[0, k].astype(F32)
            if r > 0:
                inward(k, 1).wait_recv()
                total = total + zin[1, k].astype(F32)
            zfin[k] = total.astype(BF)
            if r < Z - 1:
                outward(k, 1).start()
            if r > 0:
                outward(k, -1).start()

    def send_out(k):
        r = root(k)
        for step, beyond in ((1, z > r), (-1, z < r)):
            tip = Z - 1 if step > 0 else 0

            @pl.when(beyond)
            def _(step=step, tip=tip):
                outward(k, step).wait_recv()

                @pl.when(z != tip)
                def _():
                    outward(k, step).start()

    for task in work:
        task()
    psend_q = mm(turned[...], dall[:, 128:])
    for a in range(5):
        own_sum(a)
        for k in ((0,), (1,), (2,), (3, 4, 5, 6), (7, 8, 9, 10))[a]:
            tips(k)
    hat, scale = norm_stats(embed(hid, bound, vecs, block))
    relay_whole()

    for slot in range(9):
        for way in (0, 1):

            @pl.when(z != ends[way])
            def _(way=way, slot=slot):
                z_copy(way, z, slot, z_view(slot, z)).wait_recv()

        low = jnp.where(z == ends[0], 0.0, z_buffer(0, z, slot)[...].astype(F32))
        high = jnp.where(z == ends[1], 0.0, z_buffer(1, z, slot)[...].astype(F32))
        total = (low + high + z_view(slot, z)[...].astype(F32)).astype(BF)
        if slot < 8:
            fin[slot] = total
            dall[slot * T : (slot + 1) * T, :128] = total
        else:
            finm[...] = total
    exchange_start(fin, hkv, hk_s, hk_r)
    exchange_start(finm, hm, hm_s, hm_r)
    for k in range(7):
        partial(k)

    psend_kv = mm(turned[...], dall[:, :128])
    psend[...] = jnp.concatenate([psend_kv, psend_q], axis=1).astype(BF).reshape(S, R, 256)
    msend[...] = mm(enc_turned[...], finm[...].reshape(8 * E, 128)).astype(BF).reshape(S, R, 128)
    pgot[s] = psend[s]
    mgot[s] = msend[s]
    for d in range(1, S):
        p = (s + d) % S
        rcopy(psend.at[p], pgot.at[s], p_s.at[d], p_r.at[s], {"shard": p}).start()
        rcopy(msend.at[p], mgot.at[s], pm_s.at[d], pm_r.at[s], {"shard": p}).start()

    finish_whole()
    for k in range(7, 11):
        partial(k)
        total_of(k - 7)

    exchange_recv(dqt, hq, hq_s, hq_r)
    exchange_recv(fin, hkv, hk_s, hk_r)
    exchange_recv(finm, hm, hm_s, hm_r)
    whole.wait(0)
    whole.wait(1)
    wproj = wproj_all[...].reshape(512, 1536)
    d_query = hq[...].reshape(512, T).astype(F32).T.astype(BF)
    d_keys = jnp.concatenate([hkv[h][:, :HD] for h in range(H)], axis=1)
    d_values = jnp.concatenate([hkv[h][:, HD:] for h in range(H)], axis=1)
    d_norm = (
        mm(d_query, wproj[:, :512], 1, 1)
        + mm(d_keys, wproj[:, 512:1024], 1, 1)
        + mm(d_values, wproj[:, 1024:], 1, 1)
    )
    d_value, d_gain, d_shift = norm_back(d_norm, hat, scale, vecs[2:3, :])
    total = d_after[...] + d_value
    hidden_grad[...] = total
    pos = block * T + lax.broadcasted_iota(jnp.int32, (T, 1), 0)
    sm_mine[...] = jnp.zeros((16, 512), F32)
    sm_mine[0:1, :] = d_gain
    sm_mine[1:2, :] = small2[0:1, :]
    sm_mine[2:3, :] = small3[0:1, :]
    sm_mine[3:4, :] = d_shift
    sm_mine[4:5, :] = small2[1:2, :]
    sm_mine[5:6, :] = small3[1:2, :]
    sm_mine[6:7, :] = jnp.sum(jnp.where(pos < bound, total, 0.0), axis=0, keepdims=True)
    sm_mine[7:8, :] = jnp.sum(jnp.where(pos < bound, 0.0, total), axis=0, keepdims=True)
    sm_mine[8:9, :] = small3[2:3, :]
    for c in range(upb_g.shape[1] // 512):
        sm_mine[9 + c : 10 + c, :] = upb_g[0:1, 512 * c : 512 * (c + 1)]
    for d in range(1, S):
        rcopy(sm_mine, sm_all.at[s], sm_s.at[d], sm_r.at[s], {"shard": (s + d) % S}).start()
    sm_all[s] = sm_mine[...]

    for k in range(4, 8):
        total_of(k)

    for d in range(1, S):
        p = (s + d) % S
        rcopy(psend.at[p], pgot.at[p], p_s.at[d], p_r.at[p], {"shard": p}).wait_recv()
        rcopy(msend.at[p], mgot.at[p], pm_s.at[d], pm_r.at[p], {"shard": p}).wait_recv()
    heads, mheads = [], []
    for h in range(H):
        acc, accm = pgot[h].astype(F32), mgot[h].astype(F32)
        for g in range(1, G):
            acc = acc + pgot[8 * g + h].astype(F32)
            accm = accm + mgot[8 * g + h].astype(F32)
        heads.append(acc)
        mheads.append(accm)
    wz[11] = jnp.concatenate([v[:, 128 : 128 + HD] for v in heads], axis=1).astype(BF)
    wz[12] = jnp.concatenate([v[:, :HD] for v in heads], axis=1).astype(BF)
    wz[13] = jnp.concatenate([v[:, HD:128] for v in heads], axis=1).astype(BF)
    wz[14] = jnp.concatenate([v[:, :HD] for v in mheads], axis=1).astype(BF)
    wz[15] = jnp.concatenate([v[:, HD:] for v in mheads], axis=1).astype(BF)
    for k in range(11, NC):
        tips(k)
    e_keys = jnp.concatenate([hm[h][:, :HD] for h in range(H)], axis=1)
    e_values = jnp.concatenate([hm[h][:, HD:] for h in range(H)], axis=1)
    wmem = wmem_all[...].reshape(512, 1024)
    encoder_grad[...] = mm(e_keys, wmem[:, :512], 1, 1) + mm(e_values, wmem[:, 512:], 1, 1)

    for d in range(1, S):
        p = (s + d) % S
        rcopy(sm_mine, sm_all.at[p], sm_s.at[d], sm_r.at[p], {"shard": p}).wait_recv()
    acc = sm_all[0]
    for p in range(1, S):
        acc = acc + sm_all[p]
    sm_plane[...] = acc
    for d in range(1, Z):
        rcopy(sm_plane, sm_z.at[z], sz_s.at[d], sz_r.at[z], {"seq": (z + d) % Z}).start()
    sm_z[z] = acc
    for k in range(NC):
        if k + 11 < NC:
            partial(k + 11)
        if k + 8 < NC:
            total_of(k + 8)
        send_out(k)
    for d in range(1, Z):
        o = (z + d) % Z
        rcopy(sm_plane, sm_z.at[o], sz_s.at[d], sz_r.at[o], {"seq": o}).wait_recv()
    acc = sm_z[0]
    for o in range(1, Z):
        acc = acc + sm_z[o]
    smalls_o[...] = acc

    whole.drain()
    for a in range(5):
        for q in range(chips):
            sib_copy(a, q).wait_send()
        for d in range(1, chips):
            own_copy(a, (chip + d) % chips).wait_send()
    for d in range(1, G):
        o = (m + d) % G
        rcopy(dkv.at[o], mbuf.at[m], mb_s.at[d, 0], mb_r.at[m, 0], {"shard": o * 8 + j}).wait_send()
        rcopy(dmkv.at[o], mbufm.at[m], mb_s.at[d, 1], mb_r.at[m, 1], {"shard": o * 8 + j}).wait_send()
    exchange_sent(dqt, hq, hq_s, hq_r)
    exchange_sent(fin, hkv, hk_s, hk_r)
    exchange_sent(finm, hm, hm_s, hm_r)
    for far in range(Z - 1, 0, -1):
        for slot in range(9):
            for way in (0, 1):
                t = z + (2 * way - 1) * far

                @pl.when((t >= 0) & (t < Z))
                def _(way=way, t=t, slot=slot):
                    z_copy(way, t, slot, z_view(slot, t)).wait_send()

    for d in range(1, S):
        p = (s + d) % S
        rcopy(psend.at[p], pgot.at[s], p_s.at[d], p_r.at[s], {"shard": p}).wait_send()
        rcopy(msend.at[p], mgot.at[s], pm_s.at[d], pm_r.at[s], {"shard": p}).wait_send()
        rcopy(sm_mine, sm_all.at[s], sm_s.at[d], sm_r.at[s], {"shard": p}).wait_send()
    for d in range(1, Z):
        rcopy(sm_plane, sm_z.at[z], sz_s.at[d], sz_r.at[z], {"seq": (z + d) % Z}).wait_send()
    for k in range(NC):
        r = root(k)
        for step, beyond in ((-1, z > r), (1, z < r)):

            @pl.when(beyond)
            def _(step=step):
                inward(k, step).wait_send()

        for step in (-1, 1):
            sends = (z >= r) & (z < Z - 1) if step > 0 else (z <= r) & (z > 0)

            @pl.when(sends)
            def _(step=step):
                outward(k, step).wait_send()


def finish_kernel(
    info, timestep, zfin, sums, hid_g, enc_g, lay,
    lay_o, hid_o, enc_o, time_o, gain_o, shift_o, proj_o, out_o, cq_o, mem_o, co_o, up_o, upb_o, dn_o, dnb_o,
):
    s = info[3]
    R, F = out_o.shape[0], upb_o.shape[1]
    lay_o[...] = lay[...]
    hid_o[...] = hid_g[...]
    enc_o[...] = enc_g[...]
    out_o[...] = zfin[0].astype(F32)
    cq_o[...] = zfin[1].astype(F32)
    co_o[...] = zfin[2].astype(F32)
    for c in range(4):
        up_o[:, 512 * c : 512 * (c + 1)] = zfin[3 + c].astype(F32)
        dn_o[c * R : (c + 1) * R, :] = zfin[7 + c].astype(F32)
    for c in range(3):
        proj_o[:, 512 * c : 512 * (c + 1)] = zfin[11 + c].astype(F32)
    for c in range(2):
        mem_o[:, 512 * c : 512 * (c + 1)] = zfin[14 + c].astype(F32)

    def own(width, first):
        row = lax.broadcasted_iota(jnp.int32, (512, width), 0)
        col = lax.broadcasted_iota(jnp.int32, (512, width), 1)
        pick = jnp.where(row == col + first, 1.0, 0.0)
        return lax.dot_general(
            sums[...], pick, (((1,), (0,)), ((), ())),
            preferred_element_type=F32, precision=lax.Precision.HIGHEST,
        )

    mine = own(R, s * R)
    gain_o[...] = mine[0:3]
    shift_o[...] = mine[3:6]
    dnb_o[...] = mine[8:9]
    step = lax.broadcasted_iota(jnp.int32, time_o.shape, 0)
    grad = jnp.zeros(time_o.shape, F32)
    for d in range(DOCS):
        grad = grad + jnp.where(step == timestep[d], mine[6 + d : 7 + d], 0.0)
    time_o[...] = grad
    wide = own(F, (s * F) % 512)
    row = lax.broadcasted_iota(jnp.int32, wide.shape, 0)
    upb_o[...] = jnp.sum(jnp.where(row == 9 + s * F // 512, wide, 0.0), axis=0, keepdims=True)


def last(v):
    S, Z, G = v["S"], v["Z"], v["G"]
    T, R, F, E = v["T"], v["R"], v["F"], v["encoder"].shape[0]
    FF = v["wup"].shape[1]
    chips = S // 2
    sds = jax.ShapeDtypeStruct
    V = pltpu.VMEM
    GM, ZM = (G, Z) if G > 1 else (1, 1)
    hidden_grad, encoder_grad, zfin, sums = remote_call(
        functools.partial(last_kernel, S, Z, G),
        "gradients_home",
        4,
        (
            v["info"], v["hidden_in"], v["vecs"], v["d_after"], v["x_all"], v["enc_all"], v["dqt"],
            v["dkv"].reshape(G, 8, Z, T, 128), v["dmkv"].reshape(G, 8, Z, E, 128),
            v["self_proj"], v["cross_memory"],
            v["wout_grad"], v["cq_grad"], v["co_grad"], v["up_grad"], v["dn_grad"],
            v["small2"], v["small3"], v["upb_grad"],
        ),
        [sds((T, 512), F32), sds((E, 512), F32), sds((NC, R, 512), BF), sds((16, 512), F32)],
        [V((S, R, 1536), BF), V((S, R, 1024), BF)]
        + [V((chips, R, 512), BF)] * 3 + [V((chips, R, FF), BF), V((chips, F, 512), BF)]
        + [V((chips, R, 512), BF)] * 3 + [V((chips, R, FF), BF), V((chips, F, 512), BF)]
        + [
            V((2, Z, 8, T, 128), BF), V((2, Z, 8, E, 128), BF),
            V((8, T, 128), BF), V((8, E, 128), BF),
            V((GM, 8, ZM, T, 128), BF), V((GM, 8, ZM, E, 128), BF),
            V((8, T, 128), BF), V((8, HD, T), BF), V((8, E, 128), BF),
            V((512, 8 * T), BF), V((512, 8 * E), BF), V((8 * T, 256), BF),
            V((S, R, 256), BF), V((S, R, 256), BF), V((S, R, 128), BF), V((S, R, 128), BF),
            V((NC, R, 512), BF), V((2, NC, R, 512), BF),
            V((S, 16, 512), F32), V((Z, 16, 512), F32), V((16, 512), F32), V((16, 512), F32),
            DMA((5, chips)), DMA((5, chips)), DMA((5, chips)), DMA((5, chips)),
            DMA((2, Z, 9)), DMA((2, Z, 9)), DMA((G, 2)), DMA((G, 2)),
            DMA((8,)), DMA((8,)), DMA((8,)), DMA((8,)), DMA((8,)), DMA((8,)),
            DMA((S,)), DMA((S,)), DMA((S,)), DMA((S,)),
            DMA((2, NC)), DMA((2, NC)), DMA((2, NC)), DMA((NC,)),
            DMA((S,)), DMA((S,)), DMA((Z,)), DMA((Z,)),
        ] + Whole.scratch(2, S),
        far=(7,) if G > 1 else (),
    )
    vmem = pl.BlockSpec(memory_space=pltpu.VMEM)
    smem = pl.BlockSpec(memory_space=pltpu.SMEM)
    steps = v["time_table"].shape[0]
    outs = [
        sds((T, 512), BF), sds((T, 512), F32), sds((E, 512), F32), sds((steps, R), F32), sds((3, R), F32),
        sds((3, R), F32), sds((R, 1536), F32), sds((R, 512), F32), sds((R, 512), F32), sds((R, 1024), F32),
        sds((R, 512), F32), sds((R, FF), F32), sds((1, F), F32), sds((F, 512), F32), sds((1, R), F32),
    ]
    res = pl.pallas_call(
        finish_kernel,
        out_shape=outs,
        in_specs=[smem, smem] + [vmem] * 5,
        out_specs=[vmem] * len(outs),
        compiler_params=pltpu.CompilerParams(vmem_limit_bytes=LIMIT),
        name="outputs",
    )(v["info"], v["timestep"], zfin, sums, hidden_grad, encoder_grad, v["layer_out"])
    res = list(res)
    res[12] = res[12].reshape(F)
    res[14] = res[14].reshape(R)
    return tuple(res)


def shards(
    hidden_in, encoder, segment_ids, timestep, out_grad, time_table, norm_gain, norm_bias,
    self_proj, self_out, cross_query, cross_memory, cross_out, up_weight, up_bias, down_weight, down_bias,
):
    S, Z = lax.axis_size("shard"), lax.axis_size("seq")
    T, R, F = hidden_in.shape[0], self_proj.shape[0], up_bias.shape[0]
    G = S // 8
    info, x_all, kv, qt, mkv, enc_all, vecs, upb, gout, gcq, gco, gup, gdn = gather_call(
        S,
        Z,
        (
            timestep, segment_ids.reshape(-1, 128), hidden_in, time_table, norm_gain, norm_bias,
            up_bias[None], down_bias[None], self_proj, cross_memory, encoder,
            self_out, cross_query, cross_out, up_weight, down_weight,
        ),
    )
    wout, wcq, wco = gout.reshape(512, 512), gcq.reshape(512, 512), gco.reshape(512, 512)
    wup, wdn = gup.reshape(512, -1), gdn.reshape(-1, 512)
    kv = kv.reshape(S * Z, T, 128)
    mkv = mkv.reshape(DOCS * ENC // T, T, 128)

    ot, of, lse = attend(Z, True, info, qt, kv)
    at, after, n2, cqt = middle(Z, info, ot, hidden_in, vecs, wout, wcq)
    crt, crf, clse = attend(Z, False, info, cqt, mkv)
    layer_out, d_after2, co_grad, up_grad, dn_grad, small3, upb_grad, dct = feed(
        crt, after, vecs, upb, wco, wup, wdn, out_grad
    )
    dcqt, dmkv = attend_back(Z, False, info, cqt, mkv, dct, crf, clse)
    d_after, cq_grad, wout_grad, small2, dat = middle_back(
        dcqt, after, d_after2, n2, at, vecs, wcq, wout
    )
    dqt, dkv = attend_back(Z, True, info, qt, kv, dat, of, lse)
    return last(locals())


def solution(mesh):
    return jax.shard_map(
        shards,
        mesh=mesh,
        in_specs=(
            P(("shard", "seq"), None),
            P(("shard", "seq"), None),
            P(),
            P(),
            P(("shard", "seq"), None),
            P(None, "shard"),
            P(None, "shard"),
            P(None, "shard"),
            P("shard", None),
            P("shard", None),
            P("shard", None),
            P("shard", None),
            P("shard", None),
            P("shard", None),
            P("shard"),
            P("shard", None),
            P("shard"),
        ),
        out_specs=(
            P(("shard", "seq"), None),
            P(("shard", "seq"), None),
            P(("shard", "seq"), None),
            P(None, "shard"),
            P(None, "shard"),
            P(None, "shard"),
            P("shard", None),
            P("shard", None),
            P("shard", None),
            P("shard", None),
            P("shard", None),
            P("shard", None),
            P("shard"),
            P("shard", None),
            P("shard"),
        ),
        check_vma=False,
    )
```

time: 505 us -> 311 us (0.62)
  Pallas kernels: 473 us -> 310 us
  local copies, waits for them, and re-layouts: 19.5 us -> 1.22 us
  other arithmetic: 7.53 us -> 0 us
    pallas_call x4, Pallas kernels: 291 us -> 149 us  [remote_call(): pl.pallas_call(kernel, out_shape=outs, in_specs=in_specs, out_specs=[vmem...]
    pallas_call x1, Pallas kernels: 82.4 us -> 70.4 us  [gather_call(): pl.pallas_call(functools.partial(gather_kernel, S, Z, G), out_shape=outs,...]
    pallas_call x2, Pallas kernels: 46.7 us -> 35.2 us  [attend(): pl.pallas_call(functools.partial(attend_kernel, Z, causal), out_shape=[sd...]
    unnamed x30 -> x0, local copies, waits for them, and re-layouts: 9.96 us -> none
where the time goes in v2:
time: 311 us; the launch traced here: 312 us
  Pallas kernels  310 us (100%)
    pallas_call x4, Pallas kernels, remote_call(): pl.pallas_call(kernel, out_shape=outs, in_specs=in_specs, out_specs=[vmem...  149 us
    pallas_call x1, Pallas kernels, gather_call(): pl.pallas_call(functools.partial(gather_kernel, S, Z, G), out_shape=outs,...  70.4 us
    pallas_call x2, Pallas kernels, attend_back(): pl.pallas_call(functools.partial(attend_back_kernel, Z, causal), out_shap...  51 us
    pallas_call x2, Pallas kernels, attend(): pl.pallas_call(functools.partial(attend_kernel, Z, causal), out_shape=[sd...  35.2 us

profile of v2, /device:TPU:0, one launch (start us, length us, event | category | flops | bytes accessed | tf_op | source)
XLA Modules:
  0.0 311.6 jit_solution(131021954159271380)
XLA Ops:
  0.6 1.2 broadcast_in_dim.6.upb
  1.9 70.4 %gather_qkv.1 = (s32[4]{0:T(128)}, bf16[8,256,512]{2,1,0:T(8,128)(2,1)}, bf16[1,8,4,256,128]{4,3,2,1,0:T(8,128)(2,1)}, bf16[8,64,256]{2,1,0:T(8,128)(2,1)}, bf16...) custom-call(s32[2]{0:T(128)} %timestep.3, ...), custom_call_target="tpu_custom_call" | custom-call | tf_op jit(solution)/shard_map/gather_qkv/pallas_call | solution.py:406
  72.3 25.0 %attend_self.1 = (bf16[8,64,256]{2,1,0:T(8,128)(2,1)}, f32[8,64,256]{2,1,0:T(8,128)}, f32[8,1,256]{2,1,0:T(1,128)}) custom-call(s32[4]{0:T(128)} %get-tuple-element.74.info.bnd, bf16[8,64,256]{2,1,0:T(8,128)(2,1)} %get-tuple-element.76.qt, bf16[32,256,128]{2,1,0:T(8,128)(2,1)} %bitcast.13), custom_call_target="tpu_custom_call" | custom-call | tf_op jit(solution)/shard_map/attend_self/pallas_call | solution.py:562
  97.3 14.5 %middle.1 = (bf16[8,64,256]{2,1,0:T(8,128)(2,1)}, f32[256,512]{1,0:T(8,128)}, bf16[256,512]{1,0:T(8,128)(2,1)}, bf16[8,64,256]{2,1,0:T(8,128)(2,1)}) custom-call(s32[4]{0:T(128)} %get-tuple-element.74.info.bnd, bf16[8,64,256]{2,1,0:T(8,128)(2,1)} %get-tuple-element.78.ot, bf16[256,512]{1,0:T(8,128)(2,1)} %hid.5, f32[16,512]{1,0:T(8,128)} %get-tuple-element.75.vecs, ...), custom_call_target="tpu_custom_call" | custom-call | tf_op jit(solution)/shard_map/middle/pallas_call | solution.py:702
  111.8 10.2 %attend_cross.1 = (bf16[8,64,256]{2,1,0:T(8,128)(2,1)}, f32[8,64,256]{2,1,0:T(8,128)}, f32[8,1,256]{2,1,0:T(1,128)}) custom-call(s32[4]{0:T(128)} %get-tuple-element.74.info.bnd, bf16[8,64,256]{2,1,0:T(8,128)(2,1)} %get-tuple-element.81.qt, bf16[8,256,128]{2,1,0:T(8,128)(2,1)} %bitcast.17), custom_call_target="tpu_custom_call" | custom-call | tf_op jit(solution)/shard_map/attend_cross/pallas_call | solution.py:562
  122.0 22.4 %feed_forward.1 = (bf16[256,512]{1,0:T(8,128)(2,1)}, f32[256,512]{1,0:T(8,128)}, bf16[512,512]{1,0:T(8,128)(2,1)}, bf16[512,2048]{1,0:T(8,128)(2,1)}, bf16[2048,...) custom-call(bf16[8,64,256]{2,1,0:T(8,128)(2,1)} %get-tuple-element.83.crt, ...), custom_call_target="tpu_custom_call" | custom-call | tf_op jit(solution)/shard_map/feed_forward/pallas_call | solution.py:702
  144.4 13.9 %attend_cross_back.1 = (bf16[8,64,256]{2,1,0:T(8,128)(2,1)}, bf16[8,256,128]{2,1,0:T(8,128)(2,1)}) custom-call(s32[4]{0:T(128)} %get-tuple-element.74.info.bnd, bf16[8,64,256]{2,1,0:T(8,128)(2,1)} %get-tuple-element.81.qt, bf16[8,256,128]{2,1,0:T(8,128)(2,1)} %bitcast.18, bf16[8,64,256]{2,1,0:T(8,128)(2,1)} %get-tuple-element.89.dt, ...), custom_call_target="tpu_custom_call" | custom-call | tf_op jit(solution)/shard_map/attend_cross_back/pallas_call | solution.py:644
  158.3 14.9 %middle_back.1 = (f32[256,512]{1,0:T(8,128)}, bf16[512,512]{1,0:T(8,128)(2,1)}, bf16[512,512]{1,0:T(8,128)(2,1)}, f32[8,512]{1,0:T(8,128)}, bf16[8,64,256]{2,1,0:T(8,128)(2,1)}) custom-call(bf16[8,64,256]{2,1,0:T(8,128)(2,1)} %get-tuple-element.92.dcqt, f32[256,512]{1,0:T(8,128)} %get-tuple-element.84.after, f32[256,512]{1,0:T(8,128)} %get-tuple-element.93.d_after2, ...), custom_call_target="tpu_custom_call" | custom-call | tf_op jit(solution)/shard_map/middle_back/pallas_call | solution.py:702
  173.3 37.1 %attend_self_back.1 = (bf16[8,64,256]{2,1,0:T(8,128)(2,1)}, bf16[32,256,128]{2,1,0:T(8,128)(2,1)}) custom-call(s32[4]{0:T(128)} %get-tuple-element.74.info.bnd, bf16[8,64,256]{2,1,0:T(8,128)(2,1)} %get-tuple-element.76.qt, bf16[32,256,128]{2,1,0:T(8,128)(2,1)} %bitcast.14, bf16[8,64,256]{2,1,0:T(8,128)(2,1)} %get-tuple-element.99.dt, ...), custom_call_target="tpu_custom_call" | custom-call | tf_op jit(solution)/shard_map/attend_self_back/pallas_call | solution.py:644
  210.4 97.4 %gradients_home.1 = (f32[256,512]{1,0:T(8,128)}, f32[64,512]{1,0:T(8,128)}, bf16[16,64,512]{2,1,0:T(8,128)(2,1)}, f32[16,512]{1,0:T(8,128)}) custom-call(s32[4]{0:T(128)} %get-tuple-element.74.info.bnd, bf16[256,512]{1,0:T(8,128)(2,1)} %hid.5, f32[16,512]{1,0:T(8,128)} %get-tuple-element.75.vecs, f32[256,512]{1,0:T(8,128)} %get-tuple-element.96.d_after, ...), custom_call_target="tpu_custom_call" | custom-call | tf_op jit(solution)/shard_map/gradients_home/pallas_call | solution.py:702
  307.8 3.6 %outputs.1 = (bf16[256,512]{1,0:T(8,128)(2,1)}, f32[256,512]{1,0:T(8,128)}, f32[64,512]{1,0:T(8,128)}, f32[50,64]{1,0:T(8,128)}, f32[3,64]{1,0:T(4,128)}, /*inde...) custom-call(s32[4]{0:T(128)} %get-tuple-element.74.info.bnd, ...), custom_call_target="tpu_custom_call" | custom-call | tf_op jit(solution)/shard_map/outputs/pallas_call | solution.py:1384
